TPU v7x, 32 devices: a whole 2x2x4 slice. The times are simulated.
32 devices in a mesh: dp: 8 (over z, y), fsdp: 4 (over x, core).
Axes of the slice: x: 2, y: 2, z: 4, core: 2. Of those that a mesh axis runs over, the one named last changes fastest.
Arguments:
- tokens: bfloat16 [4, 8, 1024, 768], P(None, 'dp', 'fsdp'), may hold values from -6 to 6
- segments: int32 [4, 8, 1024], P(None, 'dp', 'fsdp'), may hold values from 0 to 7, never falling along the last dimension, each value on 1 to 512 neighbouring positions
- cotangent: bfloat16 [4, 8, 1024, 768], P(None, 'dp', 'fsdp'), may hold values from -6 to 6
- w_query: bfloat16 [768, 768], P(('dp', 'fsdp')), may hold values from -0.4375 to 0.4375
- w_key: bfloat16 [768, 768], P(('dp', 'fsdp')), may hold values from -0.21875 to 0.21875
- w_value: bfloat16 [768, 768], P(('dp', 'fsdp')), may hold values from -0.21875 to 0.21875
- w_out: bfloat16 [768, 768], P(('dp', 'fsdp')), may hold values from -0.875 to 0.875
- w_gate: bfloat16 [768, 2048], P(('dp', 'fsdp')), may hold values from -0.21875 to 0.21875
- w_up: bfloat16 [768, 2048], P(('dp', 'fsdp')), may hold values from -0.21875 to 0.21875
- w_down: bfloat16 [2048, 768], P(('dp', 'fsdp')), may hold values from -0.1875 to 0.1875
- norm_attn: bfloat16 [768], P(('dp', 'fsdp')), may hold values from 0.099609375 to 1.8984375
- norm_ffn: bfloat16 [768], P(('dp', 'fsdp')), may hold values from 0.099609375 to 1.8984375
Outputs:
- output: bfloat16 [4, 8, 1024, 768], P(None, 'dp', 'fsdp')
- grad_tokens: bfloat16 [4, 8, 1024, 768], P(None, 'dp', 'fsdp')
- grad_w_query: float32 [768, 768], P(('dp', 'fsdp'))
- grad_w_key: float32 [768, 768], P(('dp', 'fsdp'))
- grad_w_value: float32 [768, 768], P(('dp', 'fsdp'))
- grad_w_out: float32 [768, 768], P(('dp', 'fsdp'))
- grad_w_gate: float32 [768, 2048], P(('dp', 'fsdp'))
- grad_w_up: float32 [768, 2048], P(('dp', 'fsdp'))
- grad_w_down: float32 [2048, 768], P(('dp', 'fsdp'))
- grad_norm_attn: float32 [768], P(('dp', 'fsdp'))
- grad_norm_ffn: float32 [768], P(('dp', 'fsdp'))
Inputs may be any that keep to these rules, and one draw needn't show every extreme that they name: `segments`: along each sequence the numbers never fall; each of the 8 documents of a sequence holds 1 to 512 tokens, and one holds exactly 512.
All inputs are finite; a program needn't handle non-finite values.
Results may differ from a plain program's by a relative error of at most 0.015.
The roundings to bfloat16 on the way count: a program that leaves them out, or rounds other values in their place, can miss the bound.
Values may be sent and summed in bfloat16 or wider, within the bound.
No kernel may reach another device: no remote copies, remote signals or barrier semaphores. Data moves between devices by JAX's collectives and lax.ppermute only.
A program may use at most 256 MiB of HBM per device.

v0:
```python
import jax
import jax.numpy as jnp
from jax import lax
from jax.sharding import PartitionSpec as P

HEAD = 64


EPSILON = 1e-05
NEGATIVE = -1e30


def angle_tables(positions, head_dim):
    midpoint = head_dim // 2
    frequency = 10000.0 ** (-(jnp.arange(midpoint, dtype=jnp.float32) / midpoint))
    angles = positions.astype(jnp.float32)[:, None] * frequency[None, :]
    return (jnp.cos(angles), jnp.sin(angles))


def rotate(values, cosine, sine_table):
    midpoint = values.shape[-1] // 2
    leading = values[..., :midpoint]
    second = values[..., midpoint:]
    return jnp.concatenate(
        [leading * cosine - second * sine_table, second * cosine + leading * sine_table], -1
    )


def outer_sum(left_rows, right_rows):
    return lax.dot_general(
        left_rows, right_rows, (((0,), (0,)), ((), ())), preferred_element_type=jnp.float32
    )


def contract(left_rows, weight_full):
    return lax.dot_general(
        left_rows, weight_full, (((1,), (1,)), ((), ())), preferred_element_type=jnp.float32
    )


def body(
    tokens,
    segments,
    cotangent,
    w_query,
    w_key,
    w_value,
    w_out,
    w_gate,
    w_up,
    w_down,
    norm_attn,
    norm_ffn,
):
    shards = (w_query, w_key, w_value, w_out, w_gate, w_up, w_down, norm_attn, norm_ffn)
    micro_count, seq_count, local_len, model_width = tokens.shape
    row_count = seq_count * local_len
    heads_count = model_width // HEAD
    length = local_len * lax.axis_size("fsdp")
    positions_local = lax.axis_index("fsdp") * local_len + jnp.arange(local_len, dtype=jnp.int32)
    positions_all = jnp.arange(length, dtype=jnp.int32)
    cosine, sine_table = angle_tables(positions_local, HEAD)
    cosine = cosine[:, None, :]
    sine_table = sine_table[:, None, :]
    causal = positions_local[:, None] >= positions_all[None, :]
    running = None
    outputs = []
    grads_in = []
    for step_index in range(micro_count):
        gathered = (
            lax.all_gather(shards[0], ("dp", "fsdp"), axis=0, tiled=True),
            lax.all_gather(shards[1], ("dp", "fsdp"), axis=0, tiled=True),
            lax.all_gather(shards[2], ("dp", "fsdp"), axis=0, tiled=True),
            lax.all_gather(shards[3], ("dp", "fsdp"), axis=0, tiled=True),
            lax.all_gather(shards[4], ("dp", "fsdp"), axis=0, tiled=True),
            lax.all_gather(shards[5], ("dp", "fsdp"), axis=0, tiled=True),
            lax.all_gather(shards[6], ("dp", "fsdp"), axis=0, tiled=True),
            lax.all_gather(shards[7], ("dp", "fsdp"), axis=0, tiled=True),
            lax.all_gather(shards[8], ("dp", "fsdp"), axis=0, tiled=True),
        )
        (
            query_full,
            key_full,
            value_full,
            out_full,
            gate_full,
            up_full,
            down_full,
            gain_one,
            gain_two,
        ) = gathered
        inputs = tokens[step_index].astype(jnp.float32).reshape(row_count, model_width)
        seg_local = segments[step_index]
        scale_one = lax.rsqrt(jnp.mean(inputs * inputs, -1, keepdims=True) + EPSILON)
        plain_one = inputs * scale_one
        normed_one = (plain_one * gain_one.astype(jnp.float32)).astype(jnp.bfloat16)
        query_pre = jnp.dot(normed_one, query_full, preferred_element_type=jnp.float32)
        key_pre = jnp.dot(normed_one, key_full, preferred_element_type=jnp.float32)
        value_pre = jnp.dot(normed_one, value_full, preferred_element_type=jnp.float32)
        head_shape = (seq_count, local_len, heads_count, HEAD)
        query_rot = rotate(query_pre.reshape(head_shape), cosine, sine_table).astype(jnp.bfloat16)
        key_rot = rotate(key_pre.reshape(head_shape), cosine, sine_table).astype(jnp.bfloat16)
        value_low = value_pre.reshape(head_shape).astype(jnp.bfloat16)
        query_heads = jnp.transpose(query_rot, (2, 0, 1, 3))
        key_local = jnp.transpose(key_rot, (2, 0, 1, 3))
        value_local = jnp.transpose(value_low, (2, 0, 1, 3))
        key_heads, value_heads, key_segments = (
            lax.all_gather(key_local, "fsdp", axis=2, tiled=True),
            lax.all_gather(value_local, "fsdp", axis=2, tiled=True),
            lax.all_gather(seg_local, "fsdp", axis=1, tiled=True),
        )
        allowed = causal[None, :, :] & (seg_local[:, :, None] == key_segments[:, None, :])

        def head_scores(query_one, key_one):
            scores = (
                jnp.einsum("sqe,ske->sqk", query_one, key_one, preferred_element_type=jnp.float32)
                * 0.125
            )
            return jnp.where(allowed, scores, NEGATIVE)

        def forward_head(head_items):
            query_one, key_one, value_one = head_items
            scores = head_scores(query_one, key_one)
            highest = jnp.max(scores, -1, keepdims=True)
            exponent = jnp.exp(scores - highest)
            denominator = jnp.sum(exponent, -1, keepdims=True)
            attn_prob = exponent / denominator
            mixed_out = jnp.einsum(
                "sqk,ske->sqe",
                attn_prob.astype(jnp.bfloat16),
                value_one,
                preferred_element_type=jnp.float32,
            )
            return (mixed_out, highest[..., 0] + jnp.log(denominator[..., 0]))

        head_out, log_total = lax.map(forward_head, (query_heads, key_heads, value_heads))
        attended = (
            jnp.transpose(head_out, (1, 2, 0, 3))
            .reshape(row_count, model_width)
            .astype(jnp.bfloat16)
        )
        middle = inputs + jnp.dot(attended, out_full, preferred_element_type=jnp.float32)
        scale_two = lax.rsqrt(jnp.mean(middle * middle, -1, keepdims=True) + EPSILON)
        plain_two = middle * scale_two
        normed_two = (plain_two * gain_two.astype(jnp.float32)).astype(jnp.bfloat16)
        gate_pre = jnp.dot(normed_two, gate_full, preferred_element_type=jnp.float32)
        up_pre = jnp.dot(normed_two, up_full, preferred_element_type=jnp.float32)
        sigmoid_gate = jax.nn.sigmoid(gate_pre)
        activated = gate_pre * sigmoid_gate
        hidden = (activated * up_pre).astype(jnp.bfloat16)
        result = middle + jnp.dot(hidden, down_full, preferred_element_type=jnp.float32)
        outputs.append(result.astype(jnp.bfloat16).reshape(seq_count, local_len, model_width))
        back_weights = (
            lax.all_gather(shards[0], ("dp", "fsdp"), axis=0, tiled=True),
            lax.all_gather(shards[1], ("dp", "fsdp"), axis=0, tiled=True),
            lax.all_gather(shards[2], ("dp", "fsdp"), axis=0, tiled=True),
            lax.all_gather(shards[3], ("dp", "fsdp"), axis=0, tiled=True),
            lax.all_gather(shards[4], ("dp", "fsdp"), axis=0, tiled=True),
            lax.all_gather(shards[5], ("dp", "fsdp"), axis=0, tiled=True),
            lax.all_gather(shards[6], ("dp", "fsdp"), axis=0, tiled=True),
            lax.all_gather(shards[7], ("dp", "fsdp"), axis=0, tiled=True),
            lax.all_gather(shards[8], ("dp", "fsdp"), axis=0, tiled=True),
        )
        (
            query_back,
            key_back,
            value_back,
            out_back,
            gate_back,
            up_back,
            down_back,
            gain_one_b,
            gain_two_b,
        ) = back_weights
        upstream = cotangent[step_index].astype(jnp.float32).reshape(row_count, model_width)
        up_low = upstream.astype(jnp.bfloat16)
        grad_down_w = outer_sum(hidden, up_low)
        grad_hidden = contract(up_low, down_back)
        grad_gate = (
            grad_hidden * up_pre * (sigmoid_gate + gate_pre * sigmoid_gate * (1.0 - sigmoid_gate))
        ).astype(jnp.bfloat16)
        grad_upward = (grad_hidden * activated).astype(jnp.bfloat16)
        grad_gate_w = outer_sum(normed_two, grad_gate)
        grad_up_w = outer_sum(normed_two, grad_upward)
        grad_normed_two = contract(grad_gate, gate_back) + contract(grad_upward, up_back)
        grad_gain_two = jnp.sum(grad_normed_two * plain_two, 0)
        grad_plain_two = grad_normed_two * gain_two_b.astype(jnp.float32)
        grad_middle = upstream + scale_two * (
            grad_plain_two - plain_two * jnp.mean(grad_plain_two * plain_two, -1, keepdims=True)
        )
        grad_branch = grad_middle.astype(jnp.bfloat16)
        grad_out_w = outer_sum(attended, grad_branch)
        grad_attended = contract(grad_branch, out_back).astype(jnp.bfloat16)
        grad_heads = jnp.transpose(grad_attended.reshape(head_shape), (2, 0, 1, 3))

        def backward_head(head_items):
            query_one, key_one, value_one, grad_one, lse_one = head_items
            scores = head_scores(query_one, key_one)
            attn_prob = jnp.exp(scores - lse_one[..., None])
            grad_prob = jnp.einsum(
                "sqe,ske->sqk", grad_one, value_one, preferred_element_type=jnp.float32
            )
            grad_value = jnp.einsum(
                "sqk,sqe->ske",
                attn_prob.astype(jnp.bfloat16),
                grad_one,
                preferred_element_type=jnp.float32,
            )
            inner_sum = jnp.sum(attn_prob * grad_prob, -1, keepdims=True)
            grad_scores = (attn_prob * (grad_prob - inner_sum)).astype(jnp.bfloat16)
            grad_query = (
                jnp.einsum("sqk,ske->sqe", grad_scores, key_one, preferred_element_type=jnp.float32)
                * 0.125
            )
            grad_key = (
                jnp.einsum(
                    "sqk,sqe->ske", grad_scores, query_one, preferred_element_type=jnp.float32
                )
                * 0.125
            )
            return (grad_query, grad_key, grad_value)

        grad_query_h, grad_key_h, grad_value_h = lax.map(
            backward_head, (query_heads, key_heads, value_heads, grad_heads, log_total)
        )
        key_share, value_share = (
            lax.psum_scatter(
                grad_key_h.astype(jnp.bfloat16), "fsdp", scatter_dimension=2, tiled=True
            ).astype(jnp.float32),
            lax.psum_scatter(
                grad_value_h.astype(jnp.bfloat16), "fsdp", scatter_dimension=2, tiled=True
            ).astype(jnp.float32),
        )
        grad_query_rows = (
            rotate(jnp.transpose(grad_query_h, (1, 2, 0, 3)), cosine, -sine_table)
            .astype(jnp.bfloat16)
            .reshape(row_count, model_width)
        )
        grad_key_rows = (
            rotate(jnp.transpose(key_share, (1, 2, 0, 3)), cosine, -sine_table)
            .astype(jnp.bfloat16)
            .reshape(row_count, model_width)
        )
        grad_value_rows = (
            jnp.transpose(value_share, (1, 2, 0, 3))
            .astype(jnp.bfloat16)
            .reshape(row_count, model_width)
        )
        grad_query_w = outer_sum(normed_one, grad_query_rows)
        grad_key_w = outer_sum(normed_one, grad_key_rows)
        grad_value_w = outer_sum(normed_one, grad_value_rows)
        grad_normed_one = (
            contract(grad_query_rows, query_back)
            + contract(grad_key_rows, key_back)
            + contract(grad_value_rows, value_back)
        )
        grad_gain_one = jnp.sum(grad_normed_one * plain_one, 0)
        grad_plain_one = grad_normed_one * gain_one_b.astype(jnp.float32)
        grad_inputs = grad_middle + scale_one * (
            grad_plain_one - plain_one * jnp.mean(grad_plain_one * plain_one, -1, keepdims=True)
        )
        grads_in.append(grad_inputs.astype(jnp.bfloat16).reshape(seq_count, local_len, model_width))
        gradients = (
            grad_query_w,
            grad_key_w,
            grad_value_w,
            grad_out_w,
            grad_gate_w,
            grad_up_w,
            grad_down_w,
            grad_gain_one,
            grad_gain_two,
        )
        if running is None:
            running = gradients
        else:
            running = tuple(
                (
                    running_one + gradient_one
                    for running_one, gradient_one in zip(running, gradients)
                )
            )
    running = lax.psum_scatter(running, ("dp", "fsdp"), scatter_dimension=0, tiled=True)
    return (
        jnp.stack(outputs),
        jnp.stack(grads_in),
        running[0],
        running[1],
        running[2],
        running[3],
        running[4],
        running[5],
        running[6],
        running[7],
        running[8],
    )


def solution(mesh):
    placed = (
        P(None, "dp", "fsdp", None),
        P(None, "dp", "fsdp"),
        P(None, "dp", "fsdp", None),
        P(("dp", "fsdp"), None),
        P(("dp", "fsdp"), None),
        P(("dp", "fsdp"), None),
        P(("dp", "fsdp"), None),
        P(("dp", "fsdp"), None),
        P(("dp", "fsdp"), None),
        P(("dp", "fsdp"), None),
        P(("dp", "fsdp")),
        P(("dp", "fsdp")),
    )
    return jax.shard_map(
        body,
        mesh=mesh,
        in_specs=placed,
        out_specs=(
            P(None, "dp", "fsdp", None),
            P(None, "dp", "fsdp", None),
            P(("dp", "fsdp"), None),
            P(("dp", "fsdp"), None),
            P(("dp", "fsdp"), None),
            P(("dp", "fsdp"), None),
            P(("dp", "fsdp"), None),
            P(("dp", "fsdp"), None),
            P(("dp", "fsdp"), None),
            P(("dp", "fsdp")),
            P(("dp", "fsdp")),
        ),
        check_vma=False,
    )
```

profile of v0, /device:TPU:0, one launch (start us, length us, event | category | flops | bytes accessed | tf_op | source)
XLA Modules:
  0.0 2003.7 jit_solution(11688055477271379733)
XLA Ops:
  12.9 42.1 %all-reduce.5 = (bf16[768]{0:T(1024)(128)(2,1)S(1)}, bf16[768]{0:T(1024)(128)(2,1)S(1)}) all-reduce(bf16[768]{0:T(1024)(128)(2,1)S(1)} %dynamic-update-slice, bf16[768]{0:T(1024)(128)(2,1)S(1)} %dynamic-update-slice.1), channel_id=1, replica_groups=mesh['dp'=8,'fsdp'=4] {'dp','fsdp'}, use_global_device_ids=true, to_apply=%add | all-reduce | flops 1536 | bytes 6144
  69.4 54.2 %all-gather.22.cloned.1.call-done = bf16[768,768]{1,0:T(8,128)(2,1)} async-done(((bf16[24,768]{1,0:T(8,128)(2,1)}), bf16[768,768]{1,0:T(8,128)(2,1)}) %all-gather.22.cloned.1.call-update) | async-done | bytes 1179664 | tf_op jit(solution)/shard_map/all_gather | solution.py:72
  131.2 48.3 %all-gather.26.cloned.1.call-done = bf16[768,768]{1,0:T(8,128)(2,1)} async-done(((bf16[24,768]{1,0:T(8,128)(2,1)}), bf16[768,768]{1,0:T(8,128)(2,1)}) %all-gather.26.cloned.1.call-update) | async-done | bytes 1179664 | tf_op jit(solution)/shard_map/all_gather | solution.py:73
  240.9 37.8 %while.115 = (s32[]{:T(128)}, bf16[12,1,256,64]{2,3,1,0:T(8,128)(2,1)S(1)}, f32[12,1,256]{2,1,0:T(1,128)S(1)}, bf16[12,1,256,64]{3,2,1,0:T(8,128)(2,1)}, bf16[12...) while((s32[]{:T(128)}, ...), condition=%wide.region_22.23_spmd.clone, body=%wide.region_19.22_spmd.clone.sunk | while | flops 69992192 | bytes 3819633 | solution.py:136
  287.7 51.4 %while.114 = (s32[]{:T(128)}, bf16[12,1,256,64]{2,3,1,0:T(8,128)(2,1)}, f32[12,1,256]{2,1,0:T(1,128)}, bf16[12,1,256,64]{3,2,1,0:T(8,128)(2,1)}, bf16[12,1,1024,...) while((s32[]{:T(128)}, ...), condition=%wide.region_16.17_spmd.clone, body=%wide.region_13.16_spmd.clone.sunk | while | flops 69992192 | bytes 3819633 | solution.py:136
  348.0 51.5 %while.113 = (s32[]{:T(128)}, bf16[12,1,256,64]{2,3,1,0:T(8,128)(2,1)}, f32[12,1,256]{2,1,0:T(1,128)}, bf16[12,1,256,64]{3,2,1,0:T(8,128)(2,1)S(1)}, bf16[12,1,1...) while((s32[]{:T(128)}, ...), condition=%wide.region_10.11_spmd.clone, body=%wide.region_7.10_spmd.clone.sunk | while | flops 69992192 | bytes 3819633 | solution.py:136
  408.7 44.3 %while.112 = (s32[]{:T(128)}, bf16[12,1,256,64]{2,3,1,0:T(8,128)(2,1)S(1)}, f32[12,1,256]{2,1,0:T(1,128)}, bf16[12,1,256,64]{3,2,1,0:T(8,128)(2,1)S(1)}, bf16[12...) while((s32[]{:T(128)}, ...), condition=%wide.region_4.5_spmd.clone, body=%wide.region_1.4_spmd.clone.sunk | while | flops 69992192 | bytes 3819633 | solution.py:136
  471.9 56.3 %all-gather.34.cloned.1.call-done = bf16[768,2048]{1,0:T(8,128)(2,1)} async-done(((bf16[24,2048]{1,0:T(8,128)(2,1)}), bf16[768,2048]{1,0:T(8,128)(2,1)}) %all-gather.34.cloned.1.call-update) | async-done | bytes 3145744 | tf_op jit(solution)/shard_map/all_gather | solution.py:76
  532.4 56.3 %all-gather.36.cloned.1.call-done = bf16[2048,768]{1,0:T(8,128)(2,1)} async-done(((bf16[64,768]{1,0:T(8,128)(2,1)}), bf16[2048,768]{1,0:T(8,128)(2,1)}) %all-gather.36.cloned.1.call-update) | async-done | bytes 3145744 | tf_op jit(solution)/shard_map/all_gather | solution.py:77
  631.7 100.7 %while.119 = (s32[]{:T(128)}, f32[12,1,256,64]{2,3,1,0:T(8,128)}, bf16[12,1,1024,64]{2,3,1,0:T(8,128)(2,1)}, bf16[12,1,1024,64]{2,3,1,0:T(8,128)(2,1)}, bf16[12,...) while((s32[]{:T(128)}, f32[12,1,256,64]{2,3,1,0:T(8,128)}, ...), condition=%wide.region_48.49_spmd.clone, body=%wide.region_46.48_spmd.clone.sunk | while | flops 170999552 | bytes 9453705 | solution.py:223
  736.1 108.5 %while.118 = (s32[]{:T(128)}, f32[12,1,256,64]{2,3,1,0:T(8,128)}, bf16[12,1,1024,64]{2,3,1,0:T(8,128)(2,1)}, bf16[12,1,1024,64]{2,3,1,0:T(8,128)(2,1)}, bf16[12,...) while((s32[]{:T(128)}, f32[12,1,256,64]{2,3,1,0:T(8,128)}, ...), condition=%wide.region_41.42_spmd.clone, body=%wide.region_39.41_spmd.clone.sunk | while | flops 170999552 | bytes 9453705 | solution.py:223
  852.2 108.5 %while.116 = (s32[]{:T(128)}, f32[12,1,256,64]{2,3,1,0:T(8,128)}, bf16[12,1,1024,64]{2,3,1,0:T(8,128)(2,1)}, bf16[12,1,1024,64]{2,3,1,0:T(8,128)(2,1)}, bf16[12,...) while((s32[]{:T(128)}, f32[12,1,256,64]{2,3,1,0:T(8,128)}, ...), condition=%wide.region_27.28_spmd.clone, body=%wide.region_25.27_spmd.clone.sunk | while | flops 170999552 | bytes 9453705 | solution.py:223
  965.9 100.7 %while.117 = (s32[]{:T(128)}, f32[12,1,256,64]{2,3,1,0:T(8,128)}, bf16[12,1,1024,64]{2,3,1,0:T(8,128)(2,1)S(1)}, bf16[12,1,1024,64]{2,3,1,0:T(8,128)(2,1)}, bf16...) while((s32[]{:T(128)}, f32[12,1,256,64]{2,3,1,0:T(8,128)}, ...), condition=%wide.region_34.35_spmd.clone, body=%wide.region_32.34_spmd.clone.sunk | while | flops 170999552 | bytes 9453705 | solution.py:223
  1111.4 14.6 reduce-scatter.26.cloned.1.call-done
  1129.0 27.9 %reduce-scatter.18.cloned.1.call-done = bf16[12,1,256,64]{2,3,1,0:T(8,128)(2,1)} async-done(((bf16[12,1,1024,64]{2,3,1,0:T(8,128)(2,1)}), bf16[12,1,256,64]{2,3,1,0:T(8,128)(2,1)}) %reduce-scatter.18.cloned.1.call-update) | async-done | bytes 393232 | tf_op jit(solution)/shard_map/reduce_scatter | solution.py:230
  1159.9 27.7 %reduce-scatter.22.cloned.1.call-done = bf16[12,1,256,64]{2,3,1,0:T(8,128)(2,1)} async-done(((bf16[12,1,1024,64]{2,3,1,0:T(8,128)(2,1)}), bf16[12,1,256,64]{2,3,1,0:T(8,128)(2,1)}) %reduce-scatter.22.cloned.1.call-update) | async-done | bytes 393232 | tf_op jit(solution)/shard_map/reduce_scatter | solution.py:230
  1190.6 27.8 %reduce-scatter.30.cloned.1.call-done = bf16[12,1,256,64]{2,3,1,0:T(8,128)(2,1)} async-done(((bf16[12,1,1024,64]{2,3,1,0:T(8,128)(2,1)}), bf16[12,1,256,64]{2,3,1,0:T(8,128)(2,1)}) %reduce-scatter.30.cloned.1.call-update) | async-done | bytes 393232 | tf_op jit(solution)/shard_map/reduce_scatter | solution.py:230
  1275.2 40.0 %all-reduce.4 = (f32[768]{0:T(1024)S(1)}, f32[768]{0:T(1024)S(1)}) all-reduce(f32[768]{0:T(1024)S(1)} %add_add_fusion.8, f32[768]{0:T(1024)S(1)} %add_add_fusion.7), channel_id=21, replica_groups=mesh['dp'=8,'fsdp'=4] {'dp','fsdp'}, use_global_device_ids=true, to_apply=%region_63.64.clone | all-reduce | flops 1536 | bytes 12288
  1323.4 104.7 %reduce-scatter.32.cloned.1.call-done = f32[24,768]{1,0:T(8,128)} async-done(((f32[768,768]{1,0:T(8,128)}), f32[24,768]{1,0:T(8,128)}) %reduce-scatter.32.cloned.1.call-update) | async-done | bytes 73744 | tf_op jit(solution)/shard_map/reduce_scatter | solution.py:283
  1428.1 103.8 %reduce-scatter.34.cloned.1.call-done = f32[24,768]{1,0:T(8,128)} async-done(((f32[768,768]{1,0:T(8,128)}), f32[24,768]{1,0:T(8,128)}) %reduce-scatter.34.cloned.1.call-update) | async-done | bytes 73744 | tf_op jit(solution)/shard_map/reduce_scatter | solution.py:283
  1531.9 104.6 %reduce-scatter.36.cloned.1.call-done = f32[24,768]{1,0:T(8,128)} async-done(((f32[768,768]{1,0:T(8,128)}), f32[24,768]{1,0:T(8,128)}) %reduce-scatter.36.cloned.1.call-update) | async-done | bytes 73744 | tf_op jit(solution)/shard_map/reduce_scatter | solution.py:283
  1636.5 119.5 %reduce-scatter.40.cloned.1.call-done = f32[24,2048]{1,0:T(8,128)} async-done(((f32[768,2048]{1,0:T(8,128)}), f32[24,2048]{1,0:T(8,128)}) %reduce-scatter.40.cloned.1.call-update) | async-done | bytes 196624 | tf_op jit(solution)/shard_map/reduce_scatter | solution.py:283
  1756.1 120.7 %reduce-scatter.42.cloned.1.call-done = f32[24,2048]{1,0:T(8,128)} async-done(((f32[768,2048]{1,0:T(8,128)}), f32[24,2048]{1,0:T(8,128)}) %reduce-scatter.42.cloned.1.call-update) | async-done | bytes 196624 | tf_op jit(solution)/shard_map/reduce_scatter | solution.py:283
  1876.8 119.6 %reduce-scatter.44.cloned.1.call-done = f32[64,768]{1,0:T(8,128)} async-done(((f32[2048,768]{1,0:T(8,128)}), f32[64,768]{1,0:T(8,128)}) %reduce-scatter.44.cloned.1.call-update) | async-done | bytes 196624 | tf_op jit(solution)/shard_map/reduce_scatter | solution.py:283
  (1145 shorter events, 916.4 us)
Async XLA Ops:
  7.9 115.7 %all-gather.22.cloned.1.call-start = ((), (), s32[]{:S(2)}) async-start(), calls=%async_computation.16 | async-start | bytes 1216512 | tf_op jit(solution)/shard_map/all_gather | solution.py:72
  8.7 170.8 %all-gather.26.cloned.1.call-start = ((), (), s32[]{:S(2)}) async-start(), calls=%async_computation.18 | async-start | bytes 1216512 | tf_op jit(solution)/shard_map/all_gather | solution.py:73
  9.4 223.2 %all-gather.46.cloned.1.call-start = ((), (), s32[]{:S(2)}) async-start(), calls=%async_computation.28 | async-start | bytes 1966080 | tf_op jit(solution)/shard_map/all_gather | solution.py:108
  185.8 153.4 %all-gather.38.cloned.1.call-start = ((), (), s32[]{:S(2)}) async-start(), calls=%async_computation.24 | async-start | bytes 1966080 | tf_op jit(solution)/shard_map/all_gather | solution.py:108
  192.7 150.6 %all-gather.40.cloned.1.call-start = ((), (), s32[]{:S(2)}) async-start(), calls=%async_computation.25 | async-start | bytes 1966080 | tf_op jit(solution)/shard_map/all_gather | solution.py:109
  194.1 205.4 %all-gather.24.cloned.1.call-start = ((), (), s32[]{:S(2)}) async-start(), calls=%async_computation.17 | async-start | bytes 1966080 | tf_op jit(solution)/shard_map/all_gather | solution.py:108
  196.0 207.9 %all-gather.28.cloned.1.call-start = ((), (), s32[]{:S(2)}) async-start(), calls=%async_computation.19 | async-start | bytes 1966080 | tf_op jit(solution)/shard_map/all_gather | solution.py:109
  197.4 255.6 %all-gather.30.cloned.1.call-start = ((), (), s32[]{:S(2)}) async-start(), calls=%async_computation.20 | async-start | bytes 1216512 | tf_op jit(solution)/shard_map/all_gather | solution.py:74
  198.0 269.7 %all-gather.32.cloned.1.call-start = ((), (), s32[]{:S(2)}) async-start(), calls=%async_computation.21 | async-start | bytes 3244032 | tf_op jit(solution)/shard_map/all_gather | solution.py:75
  198.8 329.4 %all-gather.34.cloned.1.call-start = ((), (), s32[]{:S(2)}) async-start(), calls=%async_computation.22 | async-start | bytes 3244032 | tf_op jit(solution)/shard_map/all_gather | solution.py:76
  199.3 389.3 %all-gather.36.cloned.1.call-start = ((), (), s32[]{:S(2)}) async-start(), calls=%async_computation.23 | async-start | bytes 3244032 | tf_op jit(solution)/shard_map/all_gather | solution.py:77
  199.9 876.5 %reduce-scatter.28.cloned.1.call-start = ((), (), s32[]{:S(2)}) async-start(), calls=%async_computation.36 | async-start | bytes 1966080 | tf_op jit(solution)/shard_map/reduce_scatter | solution.py:227
  732.4 347.7 %reduce-scatter.24.cloned.1.call-start = ((), (), s32[]{:S(2)}) async-start(), calls=%async_computation.34 | async-start | bytes 1966080 | tf_op jit(solution)/shard_map/reduce_scatter | solution.py:227
  848.4 233.0 %reduce-scatter.16.cloned.1.call-start = ((), (), s32[]{:S(2)}) async-start(), calls=%async_computation.30 | async-start | bytes 1966080 | tf_op jit(solution)/shard_map/reduce_scatter | solution.py:227
  963.3 131.5 %reduce-scatter.20.cloned.1.call-start = ((), (), s32[]{:S(2)}) async-start(), calls=%async_computation.32 | async-start | bytes 1966080 | tf_op jit(solution)/shard_map/reduce_scatter | solution.py:227
  1069.0 118.6 %reduce-scatter.22.cloned.1.call-start = ((), (), s32[]{:S(2)}) async-start(), calls=%async_computation.33 | async-start | bytes 1966080 | tf_op jit(solution)/shard_map/reduce_scatter | solution.py:230
  1069.8 148.7 %reduce-scatter.30.cloned.1.call-start = ((), (), s32[]{:S(2)}) async-start(), calls=%async_computation.37 | async-start | bytes 1966080 | tf_op jit(solution)/shard_map/reduce_scatter | solution.py:230
  1070.5 252.9 %reduce-scatter.38.cloned.1.call-start = ((), (), s32[]{:S(2)}) async-start(), calls=%async_computation.41 | async-start | bytes 2433024 | tf_op jit(solution)/shard_map/reduce_scatter | solution.py:283
  1076.1 351.9 %reduce-scatter.32.cloned.1.call-start = ((), (), s32[]{:S(2)}) async-start(), calls=%async_computation.38 | async-start | bytes 2433024 | tf_op jit(solution)/shard_map/reduce_scatter | solution.py:283
  1104.5 427.5 %reduce-scatter.34.cloned.1.call-start = ((), (), s32[]{:S(2)}) async-start(), calls=%async_computation.39 | async-start | bytes 2433024 | tf_op jit(solution)/shard_map/reduce_scatter | solution.py:283
  1111.3 525.2 %reduce-scatter.36.cloned.1.call-start = ((), (), s32[]{:S(2)}) async-start(), calls=%async_computation.40 | async-start | bytes 2433024 | tf_op jit(solution)/shard_map/reduce_scatter | solution.py:283
  1223.8 532.3 %reduce-scatter.40.cloned.1.call-start = ((), (), s32[]{:S(2)}) async-start(), calls=%async_computation.42 | async-start | bytes 6488064 | tf_op jit(solution)/shard_map/reduce_scatter | solution.py:283
  1233.4 643.3 %reduce-scatter.42.cloned.1.call-start = ((), (), s32[]{:S(2)}) async-start(), calls=%async_computation.43 | async-start | bytes 6488064 | tf_op jit(solution)/shard_map/reduce_scatter | solution.py:283
  1242.4 754.0 %reduce-scatter.44.cloned.1.call-start = ((), (), s32[]{:S(2)}) async-start(), calls=%async_computation.44 | async-start | bytes 6488064 | tf_op jit(solution)/shard_map/reduce_scatter | solution.py:283
  (159 other events, 2842.6 us)
Sparse Core Ops, SparseCore 0:
  10.9 56.7 all-gather.19
  70.6 52.9 all-gather.21
  126.5 52.9 all-gather.25
  201.1 19.8 all-gather.47
  330.0 19.8 all-gather.27
  352.7 54.1 all-gather.29
  409.8 57.8 all-gather.31
  470.4 57.7 all-gather.33
  530.9 57.7 all-gather.35
  732.5 26.9 reduce-scatter.27
  848.5 26.9 reduce-scatter.23
  963.4 26.9 reduce-scatter.15
  1067.8 26.9 reduce-scatter.19
  1097.8 28.1 reduce-scatter.25
  1128.7 28.1 reduce-scatter.17
  1159.4 28.1 reduce-scatter.21
  1190.3 28.1 reduce-scatter.29
  1224.2 99.1 reduce-scatter.37
  1330.1 97.9 reduce-scatter.31
  1433.8 98.0 reduce-scatter.33
  1538.5 98.0 reduce-scatter.35
  1642.8 113.2 reduce-scatter.39
  1763.2 113.5 reduce-scatter.41
  1882.8 113.4 reduce-scatter.43
  (6 shorter events, 117.6 us)
where the time goes:
time: 2030 us; the launch traced here: 2000 us
  waiting for transfers between devices  1030 us (51%)
  matrix products  660 us (33%)
  local copies, waits for them, and re-layouts  134 us (7%)
  blocking collectives  105 us (5%)
  other arithmetic  58.3 us (3%)
    reduce_scatter x7, waiting for transfers between devices, body(): lax.psum_scatter(running, ('dp', 'fsdp'), scatter_dimension=0, tiled=True)  675 us
    dot_general x96, matrix products, head_scores(): jnp.einsum('sqe,ske->sqk', query_one, key_one, preferred_element_type=jnp...  148 us
    reduce_scatter x4, waiting for transfers between devices, body(): lax.psum_scatter(grad_value_h.astype(jnp.bfloat16), 'fsdp', scatter_dimen...  98.1 us
    dot_general x48, matrix products, backward_head(): jnp.einsum('sqk,ske->sqe', grad_scores, key_one, preferred_element_type=j...  90.3 us
    unnamed x2, blocking collectives  82.1 us
    dot_general x48, matrix products, forward_head(): jnp.einsum('sqk,ske->sqe', attn_prob.astype(jnp.bfloat16), value_one, pre...  79.3 us
    dot_general x48, matrix products, backward_head(): jnp.einsum('sqk,sqe->ske', attn_prob.astype(jnp.bfloat16), grad_one, pref...  78 us
    dot_general x48, matrix products, backward_head(): jnp.einsum('sqk,sqe->ske', grad_scores, query_one, preferred_element_type...  75.6 us
  transfers between devices with their start and end apart: 30, of which 18 were waited for; matrix products, arithmetic and copies ran while one was open for 35% of the time, Pallas kernels for 0%

commit v1 on v0

v1 whole, which is shorter than its diff:
```python
import functools
import jax, jax.numpy as jnp
from jax import lax
from jax.sharding import PartitionSpec as P
from jax.experimental import pallas as pl
from jax.experimental.pallas import tpu as pltpu
HEAD=64
EPSILON=1e-5
NEGATIVE=-1e30
TILE=256
REACH=2
VM=60*1024*1024
NT=(((1,),(1,)),((),()))
NN=(((1,),(0,)),((),()))
TN=(((0,),(0,)),((),()))
def dot(a,b,dims): return lax.dot_general(a,b,dims,preferred_element_type=jnp.float32)

def angle_tables(length):
    mid=HEAD//2
    freq=10000.0**(-(jnp.arange(mid,dtype=jnp.float32)/mid))
    ang=jnp.arange(length,dtype=jnp.int32).astype(jnp.float32)[:,None]*freq[None,:]
    c,s=jnp.cos(ang),jnp.sin(ang)
    return jnp.concatenate([c,c,c,c],1), jnp.concatenate([-s,s,-s,s],1)

def partner(v):
    lane=lax.broadcasted_iota(jnp.int32,v.shape,1)
    return jnp.where((lane % HEAD) < HEAD//2, pltpu.roll(v,v.shape[1]-HEAD//2,1), pltpu.roll(v,HEAD//2,1))

def qkv_kernel(x_ref,g_ref,cos_ref,sin_ref,wq_ref,wk_ref,wv_ref,q_ref,k_ref,v_ref,n_ref):
    x=x_ref[...].astype(jnp.float32)
    sc=lax.rsqrt(jnp.mean(x*x,-1,keepdims=True)+EPSILON)
    n=(x*sc*g_ref[...].astype(jnp.float32)).astype(jnp.bfloat16)
    n_ref[...]=n
    width=x.shape[1]
    c=cos_ref[...]; s=sin_ref[...]
    qp=dot(n,wq_ref[...],NN)
    for p in range(width//128):
        a=qp[:,128*p:128*p+128]
        r=a*c+partner(a)*s
        q_ref[:,128*p:128*p+128]=(r.astype(jnp.bfloat16).astype(jnp.float32)*0.125).astype(jnp.bfloat16)
    kp=dot(n,wk_ref[...],NN)
    for p in range(width//128):
        a=kp[:,128*p:128*p+128]
        k_ref[:,128*p:128*p+128]=(a*c+partner(a)*s).astype(jnp.bfloat16)
    v_ref[...]=dot(n,wv_ref[...],NN).astype(jnp.bfloat16)

def qkv(x,g,cos,sin,wq,wk,wv,rows=256):
    L,Dm=x.shape
    row=pl.BlockSpec((rows,Dm),lambda i:(i,0))
    tab=pl.BlockSpec((rows,128),lambda i:(i,0))
    full=pl.BlockSpec((Dm,Dm),lambda i:(0,0))
    o=jax.ShapeDtypeStruct((L,Dm),jnp.bfloat16)
    return pl.pallas_call(qkv_kernel,grid=(L//rows,),in_specs=[row,pl.BlockSpec((1,Dm),lambda i:(0,0)),tab,tab,full,full,full],
        out_specs=[row]*4,out_shape=[o]*4,name="qkv",
        compiler_params=pltpu.CompilerParams(vmem_limit_bytes=VM),
        cost_estimate=pl.CostEstimate(flops=6*L*Dm*Dm,bytes_accessed=2*(5*L*Dm+3*Dm*Dm),transcendentals=0))(x,g,cos,sin,wq,wk,wv)

def pairs(L):
    n=L//TILE
    return [(b,c) for b in range(n) for c in range(max(0,b-REACH),b+1)]

def fill_bias(bias_ref,srow_ref,scol_ref,L):
    for i,(b,c) in enumerate(pairs(L)):
        kk=lax.broadcasted_iota(jnp.int32,(TILE,TILE),0)+c*TILE
        qq=lax.broadcasted_iota(jnp.int32,(TILE,TILE),1)+b*TILE
        ok=(kk<=qq)&(scol_ref[c*TILE:c*TILE+TILE,:]==srow_ref[:,b*TILE:b*TILE+TILE])
        bias_ref[i]=jnp.where(ok,0.0,NEGATIVE)

def half(v,h):
    lane=lax.broadcasted_iota(jnp.int32,v.shape,1)
    return jnp.where((lane//HEAD)==h, v, jnp.zeros_like(v))

LOG2E=1.4426950408889634

def attn_fwd_kernel(srow_ref,scol_ref,q_ref,k_ref,v_ref,o_ref,ob_ref,lse_ref,bias_ref):
    L=q_ref.shape[0]
    @pl.when(pl.program_id(0)==0)
    def _(): fill_bias(bias_ref,srow_ref,scol_ref,L)
    idx={bc:i for i,bc in enumerate(pairs(L))}
    vt=v_ref[...].T
    for b in range(L//TILE):
        qb=q_ref[b*TILE:(b+1)*TILE,:]
        outs=[]
        cs=list(range(max(0,b-REACH),b+1))
        for h in range(2):
            qh=half(qb,h)
            ss=[dot(k_ref[c*TILE:(c+1)*TILE,:],qh,NT)+bias_ref[idx[(b,c)]] for c in cs]
            m=functools.reduce(jnp.maximum,[jnp.max(s,0,keepdims=True) for s in ss])
            ps=[jnp.exp(s-m) for s in ss]
            l=functools.reduce(lambda a,b:a+b,[jnp.sum(p,0,keepdims=True) for p in ps])
            o=functools.reduce(lambda a,b:a+b,[dot(vt[HEAD*h:HEAD*h+HEAD,c*TILE:(c+1)*TILE],p.astype(jnp.bfloat16),NN) for c,p in zip(cs,ps)])
            outs.append(o*(1.0/l))
            lse_ref[0,h:h+1,b*TILE:(b+1)*TILE]=m+jnp.log(l)
        o=jnp.concatenate(outs,0).T
        o_ref[b*TILE:(b+1)*TILE,:]=o
        ob_ref[b*TILE:(b+1)*TILE,:]=o.astype(jnp.bfloat16)

def attn_fwd(srow,scol,q,k,v):
    L,Dm=q.shape
    n=Dm//128
    blk=pl.BlockSpec((L,128),lambda p:(0,p))
    np_=len(pairs(L))
    return pl.pallas_call(attn_fwd_kernel,grid=(n,),
        in_specs=[pl.BlockSpec((1,L),lambda p:(0,0)),pl.BlockSpec((L,1),lambda p:(0,0)),blk,blk,blk],
        out_specs=[blk,blk,pl.BlockSpec((1,2,L),lambda p:(p,0,0))],
        out_shape=[jax.ShapeDtypeStruct((L,Dm),jnp.float32),jax.ShapeDtypeStruct((L,Dm),jnp.bfloat16),jax.ShapeDtypeStruct((n,2,L),jnp.float32)],
        scratch_shapes=[pltpu.VMEM((np_,TILE,TILE),jnp.float32)],name="attn_fwd",
        compiler_params=pltpu.CompilerParams(vmem_limit_bytes=VM),
        cost_estimate=pl.CostEstimate(flops=4*np_*TILE*TILE*Dm*4,bytes_accessed=12*L*Dm,transcendentals=np_*TILE*TILE*2*n))(srow,scol,q,k,v)

def attn_bwd_kernel(srow_ref,scol_ref,cos_ref,sin_ref,q_ref,k_ref,v_ref,o_ref,g_ref,lse_ref,dq_ref,dk_ref,dv_ref,bias_ref,dka_ref,dva_ref):
    L=q_ref.shape[0]
    @pl.when(pl.program_id(0)==0)
    def _(): fill_bias(bias_ref,srow_ref,scol_ref,L)
    idx={bc:i for i,bc in enumerate(pairs(L))}
    kt=k_ref[...].T
    seen=set()
    for b in range(L//TILE):
        rows=slice(b*TILE,(b+1)*TILE)
        qb=q_ref[rows,:]; gb=g_ref[rows,:]
        dt=(gb.astype(jnp.float32)*o_ref[rows,:]).T
        cs=list(range(max(0,b-REACH),b+1))
        dqs=[]
        acc={c:[None,None] for c in cs}
        for h in range(2):
            qh=half(qb,h); gh=half(gb,h)
            delta=jnp.sum(dt[HEAD*h:HEAD*h+HEAD],0,keepdims=True)
            lse=lse_ref[0,h:h+1,rows]
            dq=None
            for c in cs:
                cr=slice(c*TILE,(c+1)*TILE)
                s=dot(k_ref[cr,:],qh,NT)+bias_ref[idx[(b,c)]]
                p=jnp.exp(s-lse)
                dp=dot(v_ref[cr,:],gh,NT)
                ds=(p*(dp-delta)).astype(jnp.bfloat16)
                pv=dot(p.astype(jnp.bfloat16),gh,NN)
                dkk=dot(ds,qh,NN)
                acc[c][0]=dkk if acc[c][0] is None else acc[c][0]+dkk
                acc[c][1]=pv if acc[c][1] is None else acc[c][1]+pv
                d=dot(kt[HEAD*h:HEAD*h+HEAD,cr],ds,NN)
                dq=d if dq is None else dq+d
            dqs.append(dq)
        for c in cs:
            cr=slice(c*TILE,(c+1)*TILE)
            if c in seen:
                dka_ref[cr,:]+=acc[c][0]; dva_ref[cr,:]+=acc[c][1]
            else:
                dka_ref[cr,:]=acc[c][0]; dva_ref[cr,:]=acc[c][1]
                seen.add(c)
        dq=jnp.concatenate(dqs,0).T*0.125
        dq_ref[rows,:]=(dq*cos_ref[rows,:]-partner(dq)*sin_ref[rows,:]).astype(jnp.bfloat16)
    dk=dka_ref[...]
    dk_ref[...]=(dk*cos_ref[...]-partner(dk)*sin_ref[...]).astype(jnp.bfloat16)
    dv_ref[...]=dva_ref[...].astype(jnp.bfloat16)

def attn_bwd(srow,scol,cos,sin,q,k,v,o,g,lse):
    L,Dm=q.shape
    n=Dm//128
    blk=pl.BlockSpec((L,128),lambda p:(0,p))
    tab=pl.BlockSpec((L,128),lambda p:(0,0))
    np_=len(pairs(L))
    out=jax.ShapeDtypeStruct((L,Dm),jnp.bfloat16)
    return pl.pallas_call(attn_bwd_kernel,grid=(n,),
        in_specs=[pl.BlockSpec((1,L),lambda p:(0,0)),pl.BlockSpec((L,1),lambda p:(0,0)),tab,tab,blk,blk,blk,blk,blk,pl.BlockSpec((1,2,L),lambda p:(p,0,0))],
        out_specs=[blk]*3,out_shape=[out]*3,
        scratch_shapes=[pltpu.VMEM((np_,TILE,TILE),jnp.float32),pltpu.VMEM((L,128),jnp.float32),pltpu.VMEM((L,128),jnp.float32)],name="attn_bwd",
        compiler_params=pltpu.CompilerParams(vmem_limit_bytes=VM),
        cost_estimate=pl.CostEstimate(flops=10*np_*TILE*TILE*Dm*4,bytes_accessed=18*L*Dm,transcendentals=np_*TILE*TILE*2*n))(srow,scol,cos,sin,q,k,v,o,g,lse)


def exchange(pieces, size, axis):
    me = lax.axis_index(axis)
    own = lax.dynamic_index_in_dim(pieces, me, 0, keepdims=False)
    whole = jnp.broadcast_to(own[None], pieces.shape)
    for step in range(1, size):
        sent = lax.dynamic_index_in_dim(pieces, me ^ step, 0, keepdims=False)
        got = lax.ppermute(sent, axis, [(i, i ^ step) for i in range(size)])
        whole = lax.dynamic_update_index_in_dim(whole, got, me ^ step, 0)
    return whole


def gather(shard):
    return lax.all_gather(shard, ("dp", "fsdp"), axis=0, tiled=True)


def reduce_rows(grad):
    return lax.psum_scatter(grad.astype(jnp.bfloat16), ("dp", "fsdp"), scatter_dimension=0, tiled=True).astype(jnp.float32)


def body(tokens, segments, cotangent, w_query, w_key, w_value, w_out, w_gate, w_up, w_down, norm_attn, norm_ffn):
    f32 = jnp.float32
    bf = jnp.bfloat16
    fsdp = lax.axis_size("fsdp")
    micro, seqs, local, width = tokens.shape
    length = local * fsdp
    rows = w_query.shape[0]
    inner = w_gate.shape[1]
    gains = jnp.concatenate([norm_attn[:, None], norm_ffn[:, None], jnp.zeros((rows, 126), bf)], 1)
    head = gather(jnp.concatenate([w_query, w_key, w_value, gains], 1))
    wq, wk, wv = (head[:, i * width : (i + 1) * width] for i in range(3))
    g1, g2 = head[:, 3 * width], head[:, 3 * width + 1]
    seg_rows = jnp.pad(segments.reshape(fsdp, 1, local).astype(bf), ((0, 0), (0, 7), (0, width - local)))
    mixed = exchange(jnp.concatenate([tokens.reshape(fsdp, local, width), seg_rows], 1), fsdp, "fsdp")
    x = mixed[:, :local].reshape(length, width)
    seg = mixed[:, local, :local].reshape(length).astype(jnp.int32)
    wo = gather(w_out)
    wg = gather(w_gate)
    wu = gather(w_up)
    wd = gather(w_down)
    ct = exchange(cotangent.reshape(fsdp, local, width), fsdp, "fsdp").reshape(length, width)
    cos,sin=angle_tables(length)
    srow=seg.reshape(1, length); scol=seg.reshape(length, 1)
    q,k,v,n1=qkv(x,g1.reshape(1,width),cos,sin,wq,wk,wv)
    o,att,lse=attn_fwd(srow,scol,q,k,v)
    inputs=x.astype(f32)
    middle=inputs+dot(att,wo,NN)
    s2=lax.rsqrt(jnp.mean(middle*middle,-1,keepdims=True)+EPSILON)
    p2=middle*s2
    n2=(p2*g2.astype(f32)).astype(bf)
    gp=dot(n2,wg,NN); up=dot(n2,wu,NN)
    sg=jax.nn.sigmoid(gp); act=gp*sg
    hid=(act*up).astype(bf)
    out=(middle+dot(hid,wd,NN)).astype(bf)
    gwd=dot(hid,ct,TN)
    gh=dot(ct,wd,NT)
    gg=(gh*up*(sg+gp*sg*(1.0-sg))).astype(bf)
    gu=(gh*act).astype(bf)
    gwg=dot(n2,gg,TN); gwu=dot(n2,gu,TN)
    gn2=dot(gg,wg,NT)+dot(gu,wu,NT)
    gg2=jnp.sum(gn2*p2,0)
    gpl=gn2*g2.astype(f32)
    gm=ct.astype(f32)+s2*(gpl-p2*jnp.mean(gpl*p2,-1,keepdims=True))
    gb=gm.astype(bf)
    gwo=dot(att,gb,TN)
    ga=dot(gb,wo,NT).astype(bf)
    dq,dk,dv=attn_bwd(srow,scol,cos,sin,q,k,v,o,ga,lse)
    gwq=dot(n1,dq,TN); gwk=dot(n1,dk,TN); gwv=dot(n1,dv,TN)
    gn1=dot(dq,wq,NT)+dot(dk,wk,NT)+dot(dv,wv,NT)
    s1=lax.rsqrt(jnp.mean(inputs*inputs,-1,keepdims=True)+EPSILON)
    p1=inputs*s1
    gg1=jnp.sum(gn1*p1,0)
    gpl=gn1*g1.astype(f32)
    gx=(gm+s1*(gpl-p1*jnp.mean(gpl*p1,-1,keepdims=True))).astype(bf)

    output = exchange(out.reshape(fsdp, local, width), fsdp, "fsdp").reshape(micro, seqs, local, width)
    grad_tokens = exchange(gx.reshape(fsdp, local, width), fsdp, "fsdp").reshape(micro, seqs, local, width)
    small = lax.psum_scatter(jnp.stack([gg1, gg2], 1), ("dp", "fsdp"), scatter_dimension=0, tiled=True)
    return (output, grad_tokens, reduce_rows(gwq), reduce_rows(gwk), reduce_rows(gwv), reduce_rows(gwo),
        reduce_rows(gwg), reduce_rows(gwu), reduce_rows(gwd), small[:, 0], small[:, 1])


def solution(mesh):
    rows = P(("dp", "fsdp"), None)
    vec = P(("dp", "fsdp"))
    tok = P(None, "dp", "fsdp", None)
    return jax.shard_map(
        body,
        mesh=mesh,
        in_specs=(tok, P(None, "dp", "fsdp"), tok) + (rows,) * 7 + (vec,) * 2,
        out_specs=(tok, tok) + (rows,) * 7 + (vec,) * 2,
        check_vma=False,
    )
```

time: 2030 us -> 1080 us (0.53)
  matrix products: 660 us -> 99.8 us
  waiting for transfers between devices: 1030 us -> 753 us
  local copies, waits for them, and re-layouts: 134 us -> 63.5 us
  Pallas kernels: 0 us -> 62.5 us
  blocking collectives: 105 us -> 43 us
  other arithmetic: 58.3 us -> 21.3 us
    dot_general x420 -> x18, matrix products: 660 us -> 99.8 us  [dot(): return lax.dot_general(a, b, dims, preferred_element_type=jnp.float32)]
    reduce_scatter x15 -> x7, waiting for transfers between devices: 785 us -> 552 us  [reduce_rows(): lax.psum_scatter(grad.astype(jnp.bfloat16), ('dp', 'fsdp'), scatter_dimen...]
    all_gather x15 -> x5, waiting for transfers between devices: 234 us -> 159 us  [gather(): return lax.all_gather(shard, ('dp', 'fsdp'), axis=0, tiled=True)]
    pallas_call x0 -> x3, Pallas kernels: none -> 62.5 us  [the longest x1 31.6 us: attn_bwd(): pl.pallas_call(attn_bwd_kernel, grid=(n,), in_specs=[pl.BlockSpec((1, L),...]
    unnamed x327 -> x43, local copies, waits for them, and re-layouts: 63.8 us -> 6.67 us
    unnamed x2 -> x1, blocking collectives: 82.1 us -> 43 us
    ppermute x0 -> x12, waiting for transfers between devices: none -> 39.1 us  [exchange(): got = lax.ppermute(sent, axis, [(i, i ^ step) for i in range(size)])]
    dynamic_slice x48 -> x0, local copies, waits for them, and re-layouts: 24.8 us -> none  [body(): lax.map(backward_head, (query_heads, key_heads, value_heads, grad_heads,...]
  transfers between devices with their start and end apart: 30 -> 24, of which waited for: 18 -> 14; matrix products, arithmetic and copies ran while one was open for 35% -> 14% of each run, Pallas kernels for 0% -> 6%
where the time goes in v1:
time: 1080 us; the launch traced here: 1070 us
  waiting for transfers between devices  753 us (70%)
  matrix products  99.8 us (9%)
  local copies, waits for them, and re-layouts  63.5 us (6%)
  Pallas kernels  62.5 us (6%)
  blocking collectives  43 us (4%)
  other arithmetic  21.3 us (2%)
  between operations  14.9 us (1%)
    reduce_scatter x7, waiting for transfers between devices, reduce_rows(): lax.psum_scatter(grad.astype(jnp.bfloat16), ('dp', 'fsdp'), scatter_dimen...  552 us
    all_gather x5, waiting for transfers between devices, gather(): return lax.all_gather(shard, ('dp', 'fsdp'), axis=0, tiled=True)  159 us
    dot_general x18, matrix products, dot(): return lax.dot_general(a, b, dims, preferred_element_type=jnp.float32)  99.8 us
    unnamed x1, blocking collectives  43 us
    ppermute x12, waiting for transfers between devices, exchange(): got = lax.ppermute(sent, axis, [(i, i ^ step) for i in range(size)])  39.1 us
    dynamic_update_slice x12, local copies, waits for them, and re-layouts, exchange(): whole = lax.dynamic_update_index_in_dim(whole, got, me ^ step, 0)  36.6 us
    pallas_call x1, Pallas kernels, attn_bwd(): pl.pallas_call(attn_bwd_kernel, grid=(n,), in_specs=[pl.BlockSpec((1, L),...  31.6 us
    pallas_call x1, Pallas kernels, attn_fwd(): pl.pallas_call(attn_fwd_kernel, grid=(n,), in_specs=[pl.BlockSpec((1, L),...  22.5 us
  transfers between devices with their start and end apart: 24, of which 14 were waited for; matrix products, arithmetic and copies ran while one was open for 14% of the time, Pallas kernels for 6%

profile of v1, /device:TPU:0, one launch (start us, length us, event | category | flops | bytes accessed | tf_op | source)
XLA Modules:
  0.0 1067.6 jit_solution(11191183788859504554)
XLA Ops:
  26.0 10.8 %collective-permute-done.7 = bf16[256,768]{1,0:T(8,128)(2,1)S(1)} collective-permute-done((bf16[256,768]{1,0:T(8,128)(2,1)S(1)}, bf16[256,768]{1,0:T(8,128)(2,1)S(1)}, u32[]{:S(2)}, u32[]{:S(2)}) %collective-permute-start.7) | collective-permute-done | bytes 393248 | tf_op jit(solution)/shard_map/ppermute | solution.py:177
  38.4 9.5 collective-permute-done.2
  48.5 8.2 collective-permute-done.1
  60.1 12.7 %dynamic_update_slice.44 = bf16[4,264,768]{2,0,1:T(4,128)(2,1)S(1)} dynamic-update-slice(bf16[4,264,768]{2,0,1:T(4,128)(2,1)S(1)} %broadcast_in_dim.73, bf16[1,264,768]{2,0,1:T(2,128)(2,1)} %copy.51, s32[]{:T(128)S(6)} %select_n.41, s32[]{:T(128)} %constant.96.clone.1, s32[]{:T(128)} %constant.96.clone.1) | dynamic-update-slice | bytes 811012 | tf_op jit(solution)/shard_map/jit(dynamic_update_index_in_dim)/dynamic_update_slice | solution.py:178
  72.9 12.2 %dynamic_update_slice.45 = bf16[4,264,768]{2,0,1:T(4,128)(2,1)S(1)} dynamic-update-slice(bf16[4,264,768]{2,0,1:T(4,128)(2,1)S(1)} %dynamic_update_slice.44, bf16[1,264,768]{2,0,1:T(2,128)(2,1)} %copy.52, s32[]{:T(128)S(6)} %select_n.42, s32[]{:T(128)} %constant.96.clone.1, s32[]{:T(128)} %constant.96.clone.1) | dynamic-update-slice | bytes 811012 | tf_op jit(solution)/shard_map/jit(dynamic_update_index_in_dim)/dynamic_update_slice | solution.py:178
  100.8 8.4 qkv.1
  109.2 22.5 %attn_fwd.1 = (f32[1024,768]{1,0:T(8,128)}, bf16[1024,768]{1,0:T(8,128)(2,1)}, f32[6,2,1024]{2,1,0:T(2,128)}) custom-call(s32[1,1024]{1,0:T(1,128)} %bitcast.124, s32[1024,1]{1,0:T(8,128)} %bitcast.116, bf16[1024,768]{1,0:T(8,128)(2,1)} %get-tuple-element.21.q_ref, bf16[1024,768]{1,0:T(8,128)(2,1)} %get-tuple-element.22.k_ref, ...), custom_call_target="tpu_custom_call" | custom-call | flops 7247757312 | bytes 9437184 | tf_op jit(solution)/shard_map/attn_fwd/pallas_call | solution.py:103
  139.5 54.4 %all-gather.12.cloned.1.call-done = bf16[768,2048]{1,0:T(8,128)(2,1)} async-done(((bf16[24,2048]{1,0:T(8,128)(2,1)}), bf16[768,2048]{1,0:T(8,128)(2,1)}) %all-gather.12.cloned.1.call-update) | async-done | bytes 3145744 | tf_op jit(solution)/shard_map/all_gather | solution.py:183
  193.9 9.0 fusion.22
  202.9 51.5 %all-gather.10.cloned.1.call-done = bf16[768,2048]{1,0:T(8,128)(2,1)} async-done(((bf16[24,2048]{1,0:T(8,128)(2,1)}), bf16[768,2048]{1,0:T(8,128)(2,1)}) %all-gather.10.cloned.1.call-update) | async-done | bytes 3145744 | tf_op jit(solution)/shard_map/all_gather | solution.py:183
  254.4 9.0 fusion.21
  263.4 51.5 %all-gather.14.cloned.1.call-done = bf16[2048,768]{1,0:T(8,128)(2,1)} async-done(((bf16[64,768]{1,0:T(8,128)(2,1)}), bf16[2048,768]{1,0:T(8,128)(2,1)}) %all-gather.14.cloned.1.call-update) | async-done | bytes 3145744 | tf_op jit(solution)/shard_map/all_gather | solution.py:183
  314.9 14.0 %multiply_convert_fusion = (bf16[1024,2048]{1,0:T(8,128)(2,1)}, bf16[1024,2048]{1,0:T(8,128)(2,1)S(1)}, bf16[1024,2048]{1,0:T(8,128)(2,1)}) fusion(f32[1024,2048]{1,0:T(8,128)} %fusion.21, f32[1024,2048]{1,0:T(8,128)} %fusion.22, bf16[1024,768]{1,0:T(8,128)(2,1)} %bitcast.26, bf16[2048,768]{1,0:T(8,128)(2,1)} %all-gather.14.cloned.1.call-done), kind=kOutput, calls=%fused_computation | convolution fusion | flops 3250585600 | bytes 34078720 | tf_op jit(solution)/shard_map/dot_general | solution.py:16
  350.0 31.6 %attn_bwd.1 = (bf16[1024,768]{1,0:T(8,128)(2,1)}, bf16[1024,768]{1,0:T(8,128)(2,1)}, bf16[1024,768]{1,0:T(8,128)(2,1)}) custom-call(s32[1,1024]{1,0:T(1,128)} %bitcast.125, s32[1024,1]{1,0:T(8,128)} %bitcast.117, f32[1024,128]{1,0:T(8,128)} %get-tuple-element.68.cos_ref, f32[1024,128]{1,0:T(8,128)} %get-tuple-element.69.sin_ref, ...), custom_call_target="tpu_custom_call" | custom-call | flops 18119393280 | bytes 14155776 | tf_op jit(solution)/shard_map/attn_bwd/pallas_call | solution.py:163
  395.5 7.9 convolution_convert_fusion.1
  403.5 7.8 convolution_convert_fusion.2
  439.9 43.0 %all-reduce.1 = f32[768,2]{0,1:T(2,128)S(1)} all-reduce(f32[768,2]{0,1:T(2,128)S(1)} %pad_maximum_fusion.2), channel_id=9, replica_groups=mesh['dp'=8,'fsdp'=4] {'dp','fsdp'}, use_global_device_ids=true, to_apply=%region_13.14.clone | all-reduce | flops 1536 | bytes 12288
  483.7 10.6 collective-permute-done.11
  499.3 41.3 %reduce-scatter.9.cloned.1.call-done = bf16[24,768]{1,0:T(8,128)(2,1)} async-done(((bf16[768,768]{1,0:T(8,128)(2,1)}), bf16[24,768]{1,0:T(8,128)(2,1)}) %reduce-scatter.9.cloned.1.call-update) | async-done | bytes 36880 | tf_op jit(solution)/shard_map/reduce_scatter | solution.py:187
  542.0 99.0 %reduce-scatter.11.cloned.1.call-done = bf16[24,768]{1,0:T(8,128)(2,1)} async-done(((bf16[768,768]{1,0:T(8,128)(2,1)}), bf16[24,768]{1,0:T(8,128)(2,1)}) %reduce-scatter.11.cloned.1.call-update) | async-done | bytes 36880 | tf_op jit(solution)/shard_map/reduce_scatter | solution.py:187
  642.4 99.0 %reduce-scatter.13.cloned.1.call-done = bf16[24,768]{1,0:T(8,128)(2,1)} async-done(((bf16[768,768]{1,0:T(8,128)(2,1)}), bf16[24,768]{1,0:T(8,128)(2,1)}) %reduce-scatter.13.cloned.1.call-update) | async-done | bytes 36880 | tf_op jit(solution)/shard_map/reduce_scatter | solution.py:187
  742.8 104.5 %reduce-scatter.19.cloned.1.call-done = bf16[24,2048]{1,0:T(8,128)(2,1)} async-done(((bf16[768,2048]{1,0:T(8,128)(2,1)}), bf16[24,2048]{1,0:T(8,128)(2,1)}) %reduce-scatter.19.cloned.1.call-update) | async-done | bytes 98320 | tf_op jit(solution)/shard_map/reduce_scatter | solution.py:187
  848.9 104.3 %reduce-scatter.17.cloned.1.call-done = bf16[24,2048]{1,0:T(8,128)(2,1)} async-done(((bf16[768,2048]{1,0:T(8,128)(2,1)}), bf16[24,2048]{1,0:T(8,128)(2,1)}) %reduce-scatter.17.cloned.1.call-update) | async-done | bytes 98320 | tf_op jit(solution)/shard_map/reduce_scatter | solution.py:187
  954.8 104.3 %reduce-scatter.21.cloned.1.call-done = bf16[64,768]{1,0:T(8,128)(2,1)} async-done(((bf16[2048,768]{1,0:T(8,128)(2,1)}), bf16[64,768]{1,0:T(8,128)(2,1)}) %reduce-scatter.21.cloned.1.call-update) | async-done | bytes 98320 | tf_op jit(solution)/shard_map/reduce_scatter | solution.py:187
  (160 shorter events, 125.8 us)
Async XLA Ops:
  7.2 86.8 %all-gather.6.cloned.1.call-start = ((), (), s32[]{:S(2)}) async-start(), calls=%async_computation.7 | async-start | bytes 3852288 | tf_op jit(solution)/shard_map/all_gather | solution.py:183
  10.4 122.7 %all-gather.8.cloned.1.call-start = ((), (), s32[]{:S(2)}) async-start(), calls=%async_computation.8 | async-start | bytes 1216512 | tf_op jit(solution)/shard_map/all_gather | solution.py:183
  11.2 182.7 %all-gather.12.cloned.1.call-start = ((), (), s32[]{:S(2)}) async-start(), calls=%async_computation.10 | async-start | bytes 3244032 | tf_op jit(solution)/shard_map/all_gather | solution.py:183
  11.9 242.5 %all-gather.10.cloned.1.call-start = ((), (), s32[]{:S(2)}) async-start(), calls=%async_computation.9 | async-start | bytes 3244032 | tf_op jit(solution)/shard_map/all_gather | solution.py:183
  12.5 302.4 %all-gather.14.cloned.1.call-start = ((), (), s32[]{:S(2)}) async-start(), calls=%async_computation.11 | async-start | bytes 3244032 | tf_op jit(solution)/shard_map/all_gather | solution.py:183
  13.1 484.8 %reduce-scatter.15.cloned.1.call-start = ((), (), s32[]{:S(2)}) async-start(), calls=%async_computation.15 | async-start | bytes 1216512 | tf_op jit(solution)/shard_map/reduce_scatter | solution.py:187
  14.6 23.0 %collective-permute-start.8 = (bf16[256,768]{1,0:T(8,128)(2,1)S(1)}, bf16[256,768]{1,0:T(8,128)(2,1)S(1)}, u32[]{:S(2)}, u32[]{:S(2)}) collective-permute-start(bf16[256,768]{1,0:T(8,128)(2,1)S(1)} %get-tuple-element.51), channel_id=1, source_target_pairs={{0,3},{1,2},{2,1},{3,0},{4,7},{5,6},{6,5},{7,4},{8,11},{9,10},{10,... | collective-permute-start | bytes 1179656 | tf_op jit(solution)/shard_map/ppermute | solution.py:177
  17.0 6.9 collective-permute-start.6
  17.7 19.1 %collective-permute-start.7 = (bf16[256,768]{1,0:T(8,128)(2,1)S(1)}, bf16[256,768]{1,0:T(8,128)(2,1)S(1)}, u32[]{:S(2)}, u32[]{:S(2)}) collective-permute-start(bf16[256,768]{1,0:T(8,128)(2,1)S(1)} %get-tuple-element.54), channel_id=1, source_target_pairs={{0,2},{1,3},{2,0},{3,1},{4,6},{5,7},{6,4},{7,5},{8,10},{9,11},{10,... | collective-permute-start | bytes 1179656 | tf_op jit(solution)/shard_map/ppermute | solution.py:177
  18.0 29.8 %collective-permute-start.2 = (bf16[264,768]{1,0:T(8,128)(2,1)S(1)}, bf16[264,768]{1,0:T(8,128)(2,1)S(1)}, u32[]{:S(2)}, u32[]{:S(2)}) collective-permute-start(bf16[264,768]{1,0:T(8,128)(2,1)S(1)} %get-tuple-element.43), channel_id=1, source_target_pairs={{0,3},{1,2},{2,1},{3,0},{4,7},{5,6},{6,5},{7,4},{8,11},{9,10},{10,... | collective-permute-start | bytes 1216520 | tf_op jit(solution)/shard_map/ppermute | solution.py:177
  19.4 37.3 %collective-permute-start.1 = (bf16[264,768]{1,0:T(8,128)(2,1)S(1)}, bf16[264,768]{1,0:T(8,128)(2,1)S(1)}, u32[]{:S(2)}, u32[]{:S(2)}) collective-permute-start(bf16[264,768]{1,0:T(8,128)(2,1)S(1)} %get-tuple-element.44), channel_id=1, source_target_pairs={{0,2},{1,3},{2,0},{3,1},{4,6},{5,7},{6,4},{7,5},{8,10},{9,11},{10,... | collective-permute-start | bytes 1216520 | tf_op jit(solution)/shard_map/ppermute | solution.py:177
  23.9 34.3 %collective-permute-start = (bf16[264,768]{1,0:T(8,128)(2,1)S(1)}, bf16[264,768]{1,0:T(8,128)(2,1)S(1)}, u32[]{:S(2)}, u32[]{:S(2)}) collective-permute-start(bf16[264,768]{1,0:T(8,128)(2,1)S(1)} %get-tuple-element.45), channel_id=1, source_target_pairs={{0,1},{1,0},{2,3},{3,2},{4,5},{5,4},{6,7},{7,6},{8,9},{9,8},{10,11... | collective-permute-start | bytes 1216520 | tf_op jit(solution)/shard_map/ppermute | solution.py:177
  345.1 195.5 %reduce-scatter.9.cloned.1.call-start = ((), (), s32[]{:S(2)}) async-start(), calls=%async_computation.12 | async-start | bytes 1216512 | tf_op jit(solution)/shard_map/reduce_scatter | solution.py:187
  386.0 255.0 %reduce-scatter.11.cloned.1.call-start = ((), (), s32[]{:S(2)}) async-start(), calls=%async_computation.13 | async-start | bytes 1216512 | tf_op jit(solution)/shard_map/reduce_scatter | solution.py:187
  390.4 350.9 %reduce-scatter.13.cloned.1.call-start = ((), (), s32[]{:S(2)}) async-start(), calls=%async_computation.14 | async-start | bytes 1216512 | tf_op jit(solution)/shard_map/reduce_scatter | solution.py:187
  395.0 452.3 %reduce-scatter.19.cloned.1.call-start = ((), (), s32[]{:S(2)}) async-start(), calls=%async_computation.17 | async-start | bytes 3244032 | tf_op jit(solution)/shard_map/reduce_scatter | solution.py:187
  403.4 549.8 %reduce-scatter.17.cloned.1.call-start = ((), (), s32[]{:S(2)}) async-start(), calls=%async_computation.16 | async-start | bytes 3244032 | tf_op jit(solution)/shard_map/reduce_scatter | solution.py:187
  411.3 647.7 %reduce-scatter.21.cloned.1.call-start = ((), (), s32[]{:S(2)}) async-start(), calls=%async_computation.18 | async-start | bytes 3244032 | tf_op jit(solution)/shard_map/reduce_scatter | solution.py:187
  421.2 75.6 %collective-permute-start.5 = (bf16[256,768]{1,0:T(8,128)(2,1)}, bf16[256,768]{1,0:T(8,128)(2,1)}, u32[]{:S(2)}, u32[]{:S(2)}) collective-permute-start(bf16[256,768]{1,0:T(8,128)(2,1)} %get-tuple-element.55), channel_id=1, source_target_pairs={{0,3},{1,2},{2,1},{3,0},{4,7},{5,6},{6,5},{7,4},{8,11},{9,10},{10,... | collective-permute-start | bytes 1179656 | tf_op jit(solution)/shard_map/ppermute | solution.py:177
  422.3 73.4 %collective-permute-start.4 = (bf16[256,768]{1,0:T(8,128)(2,1)}, bf16[256,768]{1,0:T(8,128)(2,1)}, u32[]{:S(2)}, u32[]{:S(2)}) collective-permute-start(bf16[256,768]{1,0:T(8,128)(2,1)} %get-tuple-element.56), channel_id=1, source_target_pairs={{0,2},{1,3},{2,0},{3,1},{4,6},{5,7},{6,4},{7,5},{8,10},{9,11},{10,... | collective-permute-start | bytes 1179656 | tf_op jit(solution)/shard_map/ppermute | solution.py:177
  423.1 71.3 %collective-permute-start.3 = (bf16[256,768]{1,0:T(8,128)(2,1)}, bf16[256,768]{1,0:T(8,128)(2,1)}, u32[]{:S(2)}, u32[]{:S(2)}) collective-permute-start(bf16[256,768]{1,0:T(8,128)(2,1)} %get-tuple-element.57), channel_id=1, source_target_pairs={{0,1},{1,0},{2,3},{3,2},{4,5},{5,4},{6,7},{7,6},{8,9},{9,8},{10,11... | collective-permute-start | bytes 1179656 | tf_op jit(solution)/shard_map/ppermute | solution.py:177
  438.3 45.3 %collective-permute-start.10 = (bf16[256,768]{1,0:T(8,128)(2,1)}, bf16[256,768]{1,0:T(8,128)(2,1)S(1)}, u32[]{:S(2)}, u32[]{:S(2)}) collective-permute-start(bf16[256,768]{1,0:T(8,128)(2,1)} %get-tuple-element.48), channel_id=1, source_target_pairs={{0,2},{1,3},{2,0},{3,1},{4,6},{5,7},{6,4},{7,5},{8,10},{9,11},{10,... | collective-permute-start | bytes 1179656 | tf_op jit(solution)/shard_map/ppermute | solution.py:177
  439.6 43.9 %collective-permute-start.9 = (bf16[256,768]{1,0:T(8,128)(2,1)S(1)}, bf16[256,768]{1,0:T(8,128)(2,1)S(1)}, u32[]{:S(2)}, u32[]{:S(2)}) collective-permute-start(bf16[256,768]{1,0:T(8,128)(2,1)S(1)} %get-tuple-element.49), channel_id=1, source_target_pairs={{0,1},{1,0},{2,3},{3,2},{4,5},{5,4},{6,7},{7,6},{8,9},{9,8},{10,11... | collective-permute-start | bytes 1179656 | tf_op jit(solution)/shard_map/ppermute | solution.py:177
  483.5 10.8 %collective-permute-start.11 = (bf16[256,768]{1,0:T(8,128)(2,1)}, bf16[256,768]{1,0:T(8,128)(2,1)S(1)}, u32[]{:S(2)}, u32[]{:S(2)}) collective-permute-start(bf16[256,768]{1,0:T(8,128)(2,1)} %get-tuple-element.47), channel_id=1, source_target_pairs={{0,3},{1,2},{2,1},{3,0},{4,7},{5,6},{6,5},{7,4},{8,11},{9,10},{10,... | collective-permute-start | bytes 1179656 | tf_op jit(solution)/shard_map/ppermute | solution.py:177
  (19 other events, 1242.5 us)
Sparse Core Ops, SparseCore 0:
  11.5 65.7 all-gather.5
  80.2 52.8 all-gather.7
  136.0 57.8 all-gather.11
  196.6 57.7 all-gather.9
  257.1 57.7 all-gather.13
  345.3 94.9 reduce-scatter.14
  445.3 95.2 reduce-scatter.8
  545.7 95.2 reduce-scatter.10
  646.1 95.2 reduce-scatter.12
  746.7 100.5 reduce-scatter.18
  852.7 100.3 reduce-scatter.16
  958.5 100.5 reduce-scatter.20

commit v2 on v1

v2 whole, which is shorter than its diff:
```python
import functools
import math
import jax, jax.numpy as jnp
from jax import lax
from jax.sharding import PartitionSpec as P
from jax.experimental import pallas as pl
from jax.experimental.pallas import tpu as pltpu
HEAD=64
EPSILON=1e-5
NEGATIVE=-1e30
TILE=256
PARTS=2
REACH=2
VM=60*1024*1024
NT=(((1,),(1,)),((),()))
NN=(((1,),(0,)),((),()))
TN=(((0,),(0,)),((),()))
def dot(a,b,dims): return lax.dot_general(a,b,dims,preferred_element_type=jnp.float32)

def angle_tables(length):
    mid=HEAD//2
    freq=10000.0**(-(jnp.arange(mid,dtype=jnp.float32)/mid))
    ang=jnp.arange(length,dtype=jnp.int32).astype(jnp.float32)[:,None]*freq[None,:]
    c,s=jnp.cos(ang),jnp.sin(ang)
    return jnp.concatenate([c,c,c,c],1), jnp.concatenate([-s,s,-s,s],1)

def partner(v):
    lane=lax.broadcasted_iota(jnp.int32,v.shape,1)
    return jnp.where((lane % HEAD) < HEAD//2, pltpu.roll(v,v.shape[1]-HEAD//2,1), pltpu.roll(v,HEAD//2,1))

def qkv_kernel(x_ref,g_ref,cos_ref,sin_ref,w_ref,q_ref,k_ref,v_ref,n_ref):
    x=x_ref[...].astype(jnp.float32)
    sc=lax.rsqrt(jnp.mean(x*x,-1,keepdims=True)+EPSILON)
    n=(x*sc*g_ref[...].astype(jnp.float32)).astype(jnp.bfloat16)
    n_ref[...]=n
    width=x.shape[1]
    c=cos_ref[...]; s=sin_ref[...]
    per=width//PARTS
    for part in range(PARTS):
        base=3*per*part
        qp=dot(n,w_ref[:,base:base+per],NN)
        kp=dot(n,w_ref[:,base+per:base+2*per],NN)
        v_ref[:,per*part:per*part+per]=dot(n,w_ref[:,base+2*per:base+3*per],NN).astype(jnp.bfloat16)
        for p in range(per//128):
            at=slice(per*part+128*p,per*part+128*p+128)
            a=qp[:,128*p:128*p+128]
            r=a*c+partner(a)*s
            q_ref[:,at]=(r.astype(jnp.bfloat16).astype(jnp.float32)*0.125).astype(jnp.bfloat16)
            a=kp[:,128*p:128*p+128]
            k_ref[:,at]=(a*c+partner(a)*s).astype(jnp.bfloat16)

def qkv(x,g,cos,sin,wqkv,rows=256):
    L,Dm=x.shape
    row=pl.BlockSpec((rows,Dm),lambda i:(i,0))
    tab=pl.BlockSpec((rows,128),lambda i:(i,0))
    o=jax.ShapeDtypeStruct((L,Dm),jnp.bfloat16)
    return pl.pallas_call(qkv_kernel,grid=(L//rows,),in_specs=[row,pl.BlockSpec((1,Dm),lambda i:(0,0)),tab,tab,pl.BlockSpec((Dm,3*Dm),lambda i:(0,0))],
        out_specs=[row]*4,out_shape=[o]*4,name="qkv",
        compiler_params=pltpu.CompilerParams(vmem_limit_bytes=VM),
        cost_estimate=pl.CostEstimate(flops=6*L*Dm*Dm,bytes_accessed=2*(5*L*Dm+3*Dm*Dm),transcendentals=0))(x,g,cos,sin,wqkv)

def pairs(L):
    n=L//TILE
    return [(b,c) for b in range(n) for c in range(max(0,b-REACH),b+1)]

def fill_bias(bias_ref,srow_ref,scol_ref,L):
    for i,(b,c) in enumerate(pairs(L)):
        kk=lax.broadcasted_iota(jnp.int32,(TILE,TILE),0)+c*TILE
        qq=lax.broadcasted_iota(jnp.int32,(TILE,TILE),1)+b*TILE
        ok=(kk<=qq)&(scol_ref[c*TILE:c*TILE+TILE,:]==srow_ref[:,b*TILE:b*TILE+TILE])
        bias_ref[i]=jnp.where(ok,0.0,NEGATIVE)

def make_bias(srow,scol):
    L=srow.shape[1]
    return pl.pallas_call(lambda srow_ref,scol_ref,bias_ref: fill_bias(bias_ref,srow_ref,scol_ref,L),
        out_shape=jax.ShapeDtypeStruct((len(pairs(L)),TILE,TILE),jnp.float32),name="bias",
        cost_estimate=pl.CostEstimate(flops=8*L*L,bytes_accessed=2*L*L,transcendentals=0))(srow,scol)

def half(v,h):
    lane=lax.broadcasted_iota(jnp.int32,v.shape,1)
    return jnp.where((lane//HEAD)==h, v, jnp.zeros_like(v))

LOG2E=1.4426950408889634

def attn_fwd_kernel(bias_ref,q_ref,k_ref,v_ref,*refs):
    o_ref,ob_ref,lse_ref=refs[-3:]
    L=q_ref.shape[0]
    idx={bc:i for i,bc in enumerate(pairs(L))}
    vt=v_ref[...].T
    for b in range(L//TILE):
        qb=q_ref[b*TILE:(b+1)*TILE,:]
        outs=[]
        cs=list(range(max(0,b-REACH),b+1))
        for h in range(2):
            qh=half(qb,h)
            ss=[dot(k_ref[c*TILE:(c+1)*TILE,:],qh,NT)+bias_ref[idx[(b,c)]] for c in cs]
            m=functools.reduce(jnp.maximum,[jnp.max(s,0,keepdims=True) for s in ss])
            ps=[jnp.exp(s-m) for s in ss]
            l=functools.reduce(lambda a,b:a+b,[jnp.sum(p,0,keepdims=True) for p in ps])
            o=functools.reduce(lambda a,b:a+b,[dot(vt[HEAD*h:HEAD*h+HEAD,c*TILE:(c+1)*TILE],p.astype(jnp.bfloat16),NN) for c,p in zip(cs,ps)])
            outs.append(o*(1.0/l))
            lse_ref[0,h:h+1,b*TILE:(b+1)*TILE]=m+jnp.log(l)
        o=jnp.concatenate(outs,0).T
        o_ref[b*TILE:(b+1)*TILE,:]=o
        ob_ref[b*TILE:(b+1)*TILE,:]=o.astype(jnp.bfloat16)

def attn_fwd(bias,q,k,v,part,parts,before):
    L,Dm=q.shape
    n=Dm//128
    per=n//parts
    first=part*per
    blk=pl.BlockSpec((L,128),lambda p:(0,p+first))
    np_=len(pairs(L))
    return pl.pallas_call(attn_fwd_kernel,grid=(per,),
        in_specs=[pl.BlockSpec((np_,TILE,TILE),lambda p:(0,0,0)),blk,blk,blk]+[pl.BlockSpec(memory_space=pl.ANY)]*len(before),
        out_specs=[blk,blk,pl.BlockSpec((1,2,L),lambda p:(p+first,0,0))],
        out_shape=[jax.ShapeDtypeStruct((L,Dm),jnp.float32),jax.ShapeDtypeStruct((L,Dm),jnp.bfloat16),jax.ShapeDtypeStruct((n,2,L),jnp.float32)],
        input_output_aliases={4+i:i for i in range(len(before))},name="attn_fwd",
        compiler_params=pltpu.CompilerParams(vmem_limit_bytes=VM),
        cost_estimate=pl.CostEstimate(flops=4*np_*TILE*TILE*Dm*4//parts,bytes_accessed=12*L*Dm//parts,transcendentals=np_*TILE*TILE*2*per))(bias,q,k,v,*before)

def attn_bwd_kernel(bias_ref,cos_ref,sin_ref,q_ref,k_ref,v_ref,o_ref,g_ref,lse_ref,d_ref,dka_ref,dva_ref):
    L=q_ref.shape[0]
    per=d_ref.shape[1]//3
    at=pl.program_id(0)*128
    cols=[pl.ds(pl.multiple_of(at+per*i,128),128) for i in range(3)]
    idx={bc:i for i,bc in enumerate(pairs(L))}
    kt=k_ref[...].T
    seen=set()
    for b in range(L//TILE):
        rows=slice(b*TILE,(b+1)*TILE)
        qb=q_ref[rows,:]; gb=g_ref[rows,:]
        dt=(gb.astype(jnp.float32)*o_ref[rows,:]).T
        cs=list(range(max(0,b-REACH),b+1))
        dqs=[]
        acc={c:[None,None] for c in cs}
        for h in range(2):
            qh=half(qb,h); gh=half(gb,h)
            delta=jnp.sum(dt[HEAD*h:HEAD*h+HEAD],0,keepdims=True)
            lse=lse_ref[0,h:h+1,rows]
            dq=None
            for c in cs:
                cr=slice(c*TILE,(c+1)*TILE)
                s=dot(k_ref[cr,:],qh,NT)+bias_ref[idx[(b,c)]]
                p=jnp.exp(s-lse)
                dp=dot(v_ref[cr,:],gh,NT)
                ds=(p*(dp-delta)).astype(jnp.bfloat16)
                pv=dot(p.astype(jnp.bfloat16),gh,NN)
                dkk=dot(ds,qh,NN)
                acc[c][0]=dkk if acc[c][0] is None else acc[c][0]+dkk
                acc[c][1]=pv if acc[c][1] is None else acc[c][1]+pv
                d=dot(kt[HEAD*h:HEAD*h+HEAD,cr],ds,NN)
                dq=d if dq is None else dq+d
            dqs.append(dq)
        for c in cs:
            cr=slice(c*TILE,(c+1)*TILE)
            if c in seen:
                dka_ref[cr,:]+=acc[c][0]; dva_ref[cr,:]+=acc[c][1]
            else:
                dka_ref[cr,:]=acc[c][0]; dva_ref[cr,:]=acc[c][1]
                seen.add(c)
        dq=jnp.concatenate(dqs,0).T*0.125
        d_ref[rows,cols[0]]=(dq*cos_ref[rows,:]-partner(dq)*sin_ref[rows,:]).astype(jnp.bfloat16)
    dk=dka_ref[...]
    d_ref[:,cols[1]]=(dk*cos_ref[...]-partner(dk)*sin_ref[...]).astype(jnp.bfloat16)
    d_ref[:,cols[2]]=dva_ref[...].astype(jnp.bfloat16)

def attn_bwd(bias,cos,sin,q,k,v,o,g,lse,part,parts):
    L,Dm=q.shape
    n=Dm//128
    per=n//parts
    first=part*per
    blk=pl.BlockSpec((L,128),lambda p:(0,p+first))
    tab=pl.BlockSpec((L,128),lambda p:(0,0))
    np_=len(pairs(L))
    cols=3*Dm//parts
    return pl.pallas_call(attn_bwd_kernel,grid=(per,),
        in_specs=[pl.BlockSpec((np_,TILE,TILE),lambda p:(0,0,0)),tab,tab,blk,blk,blk,blk,blk,pl.BlockSpec((1,2,L),lambda p:(p+first,0,0))],
        out_specs=pl.BlockSpec((L,cols),lambda p:(0,0)),out_shape=jax.ShapeDtypeStruct((L,cols),jnp.bfloat16),
        scratch_shapes=[pltpu.VMEM((L,128),jnp.float32),pltpu.VMEM((L,128),jnp.float32)],name="attn_bwd",
        compiler_params=pltpu.CompilerParams(vmem_limit_bytes=VM),
        cost_estimate=pl.CostEstimate(flops=10*np_*TILE*TILE*Dm*4//parts,bytes_accessed=18*L*Dm//parts,transcendentals=np_*TILE*TILE*2*per))(bias,cos,sin,q,k,v,o,g,lse)

LOW = jnp.bfloat16
SWAP = [(0, 1), (1, 0)]


def after(value, *others):
    return lax.optimization_barrier((value,) + tuple(others))[0]


def swap(value, axis):
    return lax.ppermute(value, axis, SWAP)


def exchange(pieces, axes):
    return lax.all_to_all(pieces, axes, 0, 0, tiled=True)


def exchange_start(pieces, axes):
    size = math.prod(lax.axis_size(a) for a in axes)
    me = lax.axis_index(axes)
    parts = []
    for step in range(size):
        sent = lax.dynamic_index_in_dim(pieces, me ^ step, 0, keepdims=True)
        parts.append(sent if step == 0 else lax.ppermute(sent, axes, [(i, i ^ step) for i in range(size)]))
    return parts


def exchange_end(parts, axes):
    me = lax.axis_index(axes)
    order = jnp.stack([me ^ step for step in range(len(parts))]).astype(jnp.int32)
    return place(parts, order, [parts[0].shape[2]])[0]


def copies(value, count):
    return jnp.broadcast_to(value[None], (count,) + value.shape)


def place_kernel(counts, widths, order_ref, *refs):
    ins = refs[: len(counts)]
    outs = refs[len(counts) :]
    at = 0
    for ref, count in zip(ins, counts):

        def move(i, carry, ref=ref, at=at):
            where = order_ref[at + i]
            left = 0
            for out, width in zip(outs, widths):
                out[where] = ref[i, :, left : left + width]
                left += width
            return carry

        lax.fori_loop(0, count, move, 0)
        at += count


def place(arrays, order, widths):
    counts = [a.shape[0] for a in arrays]
    rows = arrays[0].shape[1]
    total = sum(counts)
    moved = 4 * total * rows * sum(widths)
    return pl.pallas_call(
        functools.partial(place_kernel, counts, widths),
        in_specs=[pl.BlockSpec(memory_space=pltpu.SMEM)] + [pl.BlockSpec(memory_space=pltpu.VMEM)] * len(arrays),
        out_specs=[pl.BlockSpec(memory_space=pltpu.VMEM)] * len(widths),
        out_shape=[jax.ShapeDtypeStruct((total, rows, width), arrays[0].dtype) for width in widths],
        name="place",
        compiler_params=pltpu.CompilerParams(vmem_limit_bytes=VM),
        cost_estimate=pl.CostEstimate(flops=0, bytes_accessed=moved, transcendentals=0),
    )(order, *arrays)


def block_order(digits):
    strides = {"c": 1, "x": 2, "y": 2 * lax.axis_size("x"), "z": 4 * lax.axis_size("x")}
    sources = jnp.zeros((1,), jnp.int32)
    for axis, relative in digits:
        size = lax.axis_size(axis)
        mine = lax.axis_index(axis)
        part = [((mine - step) % size if relative else step) * strides[axis] for step in range(size)]
        sources = jnp.concatenate([sources + p for p in part])
    return sources.astype(jnp.int32)


def both_cores(arrays, order, widths, hold=()):
    arrays = [after(v, *hold) for v in arrays]
    arrays = arrays + [swap(v, "c") for v in arrays]
    return [v.reshape(-1, v.shape[-1]) for v in place(arrays, order, widths)]


def add_all(values):
    return functools.reduce(lambda a, b: a + b, values)


def pick(v, axis, at):
    return lax.dynamic_index_in_dim(v, at, axis, keepdims=False)


def shift(value, axis, step):
    size = lax.axis_size(axis)
    return lax.ppermute(value, axis, [(i, (i + step) % size) for i in range(size)])


def swap_plane(value, dy, dx):
    if dy and dx:
        return lax.ppermute(value, ("y", "x"), [(0, 3), (1, 2), (2, 1), (3, 0)])
    return swap(value, "y" if dy else "x")


def wide(values):
    return [v.astype(jnp.float32) for v in values]


class Reduction:
    def __init__(self, grads):
        sizes = [lax.axis_size(a) for a in "zyxc"]
        self.y, self.x, self.core = (lax.axis_index(a) for a in "yxc")
        self.split = [g.reshape(*sizes, g.shape[0] // math.prod(sizes), g.shape[1]) for g in grads]
        self.came = swap(jnp.concatenate([pick(g, 3, 1 - self.core).astype(LOW) for g in self.split], -1), "c")

    def chip(self, picks):
        own, came = [pick(g, 3, self.core) for g in self.split], self.came
        for axis, at in picks:
            own, came = [pick(g, axis, at) for g in own], pick(came, axis, at)
        return jnp.concatenate(wide(own), -1) + came.astype(jnp.float32)

    def plane(self, hold=()):
        quarter = lambda dy, dx: self.chip([(2, self.x ^ dx), (1, self.y ^ dy)])
        moves = [(0, 1), (1, 0), (1, 1)]
        self.ready = [after(quarter(*m).astype(LOW), *hold) for m in moves]
        self.parts = [quarter(0, 0)] + [swap_plane(v, *m) for v, m in zip(self.ready, moves)]

    def along(self, hold=()):
        self.row = self.chip([(1, self.y)])
        self.ready = after(self.chip([(1, 1 - self.y)]).astype(LOW), *hold)
        self.arrived = swap(self.ready, "y")

    def across(self, hold=()):
        part = lambda at: pick(self.row, 1, at) + pick(self.arrived, 1, at).astype(jnp.float32)
        self.parts = [part(self.x), swap(after(part(1 - self.x).astype(LOW), *hold), "x")]

    def across_first(self, hold=()):
        self.row = self.chip([(2, self.x)])
        self.ready = after(self.chip([(2, 1 - self.x)]).astype(LOW), *hold)
        self.arrived = swap(self.ready, "x")

    def along_last(self, hold=()):
        part = lambda at: pick(self.row, 1, at) + pick(self.arrived, 1, at).astype(jnp.float32)
        self.parts = [part(self.y), swap(after(part(1 - self.y).astype(LOW), *hold), "y")]


def deep(reductions):
    sums = jnp.concatenate([add_all(wide(r.parts)) for r in reductions], -1)
    out = exchange(sums.astype(LOW), "z")
    return [out[i : i + 1] for i in range(out.shape[0])]


def deep_shifts(reductions):
    size, me = lax.axis_size("z"), lax.axis_index("z")
    part = lambda step: jnp.concatenate([add_all([pick(v, 0, (me + step) % size).astype(jnp.float32) for v in r.parts]) for r in reductions], -1)
    return [part(0)[None]] + [shift(part(step).astype(LOW)[None], "z", step) for step in range(1, size)]


def finish(parts, left, width):
    return add_all([v[0, :, left : left + width].astype(jnp.float32) for v in parts])


def body(tokens, segments, cotangent, w_query, w_key, w_value, w_out, w_gate, w_up, w_down, norm_attn, norm_ffn):
    f32 = jnp.float32
    bf = jnp.bfloat16
    fsdp = lax.axis_size("x") * lax.axis_size("c")
    micro, seqs, local, width = tokens.shape
    length = local * fsdp
    inner = w_gate.shape[1]
    rows = w_query.shape[0]
    per = width // PARTS
    planes = lax.axis_size("z")
    head_order = block_order([("z", False), ("x", True), ("y", True), ("c", True)])
    xyc = block_order([("z", False), ("x", True), ("y", True), ("c", True)])
    yxc = block_order([("z", False), ("y", True), ("x", True), ("c", True)])
    gains = jnp.concatenate([norm_attn[:, None], norm_ffn[:, None], jnp.zeros((rows, 126), bf)], 1)
    parts = [w[:, i * per : (i + 1) * per] for i in range(PARTS) for w in (w_query, w_key, w_value)]
    head_z = exchange(copies(jnp.concatenate(parts + [gains], 1), planes), "z")
    seg_rows = jnp.pad(segments.reshape(fsdp, 1, local).astype(bf), ((0, 0), (0, 7), (0, width - local)))
    mixed = exchange_start(jnp.concatenate([tokens.reshape(fsdp, local, width), seg_rows], 1), ("x", "c"))
    head_xy = [swap_plane(head_z, *m) for m in ((0, 1), (1, 0), (1, 1))]
    gate_z = exchange(copies(after(jnp.concatenate([w_out, w_gate], 1), head_z), planes), "z")
    up_copies = copies(after(w_up, gate_z), planes)
    wqkv, gains = both_cores([head_z] + head_xy, head_order, [3 * width, 128], (up_copies,))
    up_z = exchange(up_copies, "z")
    g1, g2 = gains[:, 0], gains[:, 1]
    mixed = exchange_end(mixed, ("x", "c"))
    x = mixed[:, :local].reshape(length, width)
    seg = mixed[:, local, :local].reshape(length).astype(jnp.int32)
    gate_x = swap(after(gate_z, *head_xy), "x")
    up_y = swap(after(up_z, *head_xy), "y")
    cos, sin = angle_tables(length)
    bias = make_bias(seg.reshape(1, length), seg.reshape(length, 1))
    q, k, v, n1 = qkv(x, g1.reshape(1, width), cos, sin, wqkv)
    gate_zx = jnp.concatenate([gate_z, after(gate_x, q)], 0)
    up_zy = jnp.concatenate([up_z, after(up_y, q)], 0)
    gate_y = swap(gate_zx, "y")
    up_x = swap(up_zy, "x")
    down_z = exchange(copies(after(w_down, up_z, q), planes), "z")
    fwd = attn_fwd(bias, after(q, gate_zx, up_zy), k, v, 0, PARTS, ())
    down_x = swap(after(down_z, fwd[0]), "x")
    o, att, lse = attn_fwd(bias, q, k, v, 1, PARTS, fwd)
    down_zx = jnp.concatenate([down_z, after(down_x, o)], 0)
    down_y = swap(down_zx, "y")
    wo, wg = both_cores([gate_zx, after(gate_y, o)], xyc, [width, inner])
    (wu,) = both_cores([up_zy, after(up_x, o)], yxc, [inner])
    ct = exchange(after(cotangent, o).reshape(fsdp, local, width), ("x", "c")).reshape(length, width)
    inputs = x.astype(f32)
    middle = inputs + dot(att, wo, NN)
    s2 = lax.rsqrt(jnp.mean(middle * middle, -1, keepdims=True) + EPSILON)
    p2 = middle * s2
    n2 = (p2 * g2.astype(f32)).astype(bf)
    up = dot(n2, wu, NN)
    gp = dot(after(n2, up), wg, NN)
    sg = jax.nn.sigmoid(gp)
    act = gp * sg
    hid = (act * up).astype(bf)
    (wd,) = both_cores([down_zx, after(down_y, up)], xyc, [width])
    gwd = dot(hid, ct, TN).astype(bf)
    red_down = Reduction([gwd])
    gh = dot(ct, wd, NT)
    gg = (gh * up * (sg + gp * sg * (1.0 - sg))).astype(bf)
    gu = (gh * act).astype(bf)
    out = (middle + dot(hid, after(wd, gg), NN)).astype(bf)
    gg_later = after(gg, red_down.came)
    red_down.along()
    output = exchange(out.reshape(fsdp, local, width), ("x", "c"))
    gwg = dot(n2, gg_later, TN).astype(bf)
    red_gate = Reduction([gwg])
    gwu = dot(n2, after(gu, gwg), TN).astype(bf)
    gn2 = dot(after(gg, gwg, gwu), wg, NT) + dot(gu, wu, NT)
    gg2 = jnp.sum(gn2 * p2, 0)
    gpl = gn2 * g2.astype(f32)
    gm = ct.astype(f32) + s2 * (gpl - p2 * jnp.mean(gpl * p2, -1, keepdims=True))
    gb = gm.astype(bf)
    gwo = dot(att, after(gb, red_gate.came, red_down.arrived), TN).astype(bf)
    red_up = Reduction([gwo, gwu])
    red_down.across()
    red_gate.along()
    ga = dot(after(gb, gwo), wo, NT).astype(bf)
    ga = after(ga, red_up.came)
    red_up.across_first()
    d0 = attn_bwd(bias, cos, sin, q, k, v, o, ga, lse, 0, PARTS)
    d0_ready = after(d0, red_gate.arrived, red_up.arrived, output, *red_down.parts)
    down_parts = deep([red_down])
    red_gate.across()
    red_up.along_last()
    gw0 = dot(n1, d0_ready, TN).astype(bf)
    red_h0 = Reduction([gw0])
    gn1 = dot(after(d0, gw0), wqkv[:, : 3 * per], NT)
    red_h0.plane()
    ga = after(ga, gn1, *red_h0.ready)
    d1 = attn_bwd(bias, cos, sin, q, k, v, o, ga, lse, 1, PARTS)
    d1 = after(d1, *red_gate.parts, *red_up.parts, *red_h0.parts, *down_parts)
    ffn_parts = deep_shifts([red_gate, red_up, red_h0])
    left = 2 * inner + width
    r_down = finish(down_parts, 0, width)
    gn1 = gn1 + dot(d1, wqkv[:, 3 * per :], NT)
    s1 = lax.rsqrt(jnp.mean(inputs * inputs, -1, keepdims=True) + EPSILON)
    p1 = inputs * s1
    gg1 = jnp.sum(gn1 * p1, 0)
    small = jnp.pad(jnp.stack([gg1, gg2], 1), ((0, 0), (0, 126)))
    gpl = gn1 * g1.astype(f32)
    gx = (gm + s1 * (gpl - p1 * jnp.mean(gpl * p1, -1, keepdims=True))).astype(bf)
    grad_tokens = exchange(gx.reshape(fsdp, local, width), ("x", "c"))
    gw1 = dot(n1, after(d1, gx), TN).astype(bf)
    red_h1 = Reduction([gw1, small])
    red_h1.plane()
    h1_parts = deep_shifts([red_h1])
    heads = [jnp.concatenate([finish(ffn_parts, left + i * per, per), finish(h1_parts, i * per, per)], 1) for i in range(3)]
    return (
        output.reshape(micro, seqs, local, width),
        grad_tokens.reshape(micro, seqs, local, width),
        *heads,
        finish(ffn_parts, inner, width),
        finish(ffn_parts, 0, inner),
        finish(ffn_parts, inner + width, inner),
        r_down,
        finish(h1_parts, 3 * per, 128)[:, 0],
        finish(h1_parts, 3 * per, 128)[:, 1],
    )


def solution(mesh):
    dp, fsdp = mesh.shape["dp"], mesh.shape["fsdp"]
    fine = jax.sharding.Mesh(mesh.devices.reshape(dp // 2, 2, fsdp // 2, 2), ("z", "y", "x", "c"))
    every = ("z", "y", "x", "c")
    rows = P(every, None)
    vec = P(every)
    tok = P(None, ("z", "y"), ("x", "c"), None)
    return jax.shard_map(
        body,
        mesh=fine,
        in_specs=(tok, P(None, ("z", "y"), ("x", "c")), tok) + (rows,) * 7 + (vec,) * 2,
        out_specs=(tok, tok) + (rows,) * 7 + (vec,) * 2,
        check_vma=False,
    )
```

time: 1080 us -> 422 us (0.39)
  waiting for transfers between devices: 753 us -> 69.1 us
  starting transfers between devices: 9.88 us -> 77.9 us
  blocking collectives: 43 us -> 0 us
  Pallas kernels: 62.5 us -> 93.5 us
  other arithmetic: 21.3 us -> 49.8 us
  matrix products: 99.8 us -> 78.4 us
  local copies, waits for them, and re-layouts: 63.5 us -> 43.8 us
  between operations: 14.9 us -> 1.82 us
    reduce_scatter x7 -> x0, waiting for transfers between devices: 552 us -> none  [reduce_rows(): lax.psum_scatter(grad.astype(jnp.bfloat16), ('dp', 'fsdp'), scatter_dimen...]
    all_gather x5 -> x0, waiting for transfers between devices: 159 us -> none  [gather(): return lax.all_gather(shard, ('dp', 'fsdp'), axis=0, tiled=True)]
    unnamed x1 -> x0, blocking collectives: 43 us -> none
    all_to_all x0 -> x8, starting transfers between devices: none -> 38.8 us  [exchange(): return lax.all_to_all(pieces, axes, 0, 0, tiled=True)]
    dynamic_update_slice x12 -> x0, local copies, waits for them, and re-layouts: 36.6 us -> none  [exchange(): whole = lax.dynamic_update_index_in_dim(whole, got, me ^ step, 0)]
    ppermute x12 -> x45, starting transfers between devices: 8.76 us -> 39 us  [the longest x33 17 us: swap(): return lax.ppermute(value, axis, SWAP)]
    pallas_call x2 -> x10, Pallas kernels: 54.1 us -> 84.3 us  [the longest x2 36.4 us: attn_bwd(): pl.pallas_call(attn_bwd_kernel, grid=(per,), in_specs=[pl.BlockSpec((np_,...]
    dot_general x18 -> x16, matrix products: 99.8 us -> 78.4 us  [dot(): return lax.dot_general(a, b, dims, preferred_element_type=jnp.float32)]
  transfers between devices with their start and end apart: 24 -> 53, of which waited for: 14 -> 15; matrix products, arithmetic and copies ran while one was open for 14% -> 27% of each run, Pallas kernels for 6% -> 23%
where the time goes in v2:
time: 422 us; the launch traced here: 414 us
  Pallas kernels  93.5 us (22%)
  matrix products  78.4 us (19%)
  starting transfers between devices  77.9 us (18%)
  waiting for transfers between devices  69.1 us (16%)
  other arithmetic  49.8 us (12%)
  local copies, waits for them, and re-layouts  43.8 us (10%)
    dot_general x16, matrix products, dot(): return lax.dot_general(a, b, dims, preferred_element_type=jnp.float32)  78.4 us
    all_to_all x8, starting transfers between devices, exchange(): return lax.all_to_all(pieces, axes, 0, 0, tiled=True)  38.8 us
    pallas_call x2, Pallas kernels, attn_bwd(): pl.pallas_call(attn_bwd_kernel, grid=(per,), in_specs=[pl.BlockSpec((np_,...  36.4 us
    ppermute x33, waiting for transfers between devices, swap(): return lax.ppermute(value, axis, SWAP)  36.4 us
    pallas_call x2, Pallas kernels, attn_fwd(): pl.pallas_call(attn_fwd_kernel, grid=(per,), in_specs=[pl.BlockSpec((np_,...  25.5 us
    all_to_all x8, waiting for transfers between devices, exchange(): return lax.all_to_all(pieces, axes, 0, 0, tiled=True)  20.4 us
    pallas_call x5, Pallas kernels, place(): pl.pallas_call(functools.partial(place_kernel, counts, widths), in_specs=...  19.6 us
    ppermute x33, starting transfers between devices, swap(): return lax.ppermute(value, axis, SWAP)  17 us
  transfers between devices with their start and end apart: 53, of which 15 were waited for; matrix products, arithmetic and copies ran while one was open for 27% of the time, Pallas kernels for 23%

profile of v2, /device:TPU:0, one launch (start us, length us, event | category | flops | bytes accessed | tf_op | source)
XLA Modules:
  0.0 414.4 jit_solution(7021208398971889218)
XLA Ops:
  4.7 6.3 %all-to-all-start = ((bf16[4,24,2432]{2,1,0:T(8,128)(2,1)}), bf16[4,24,2432]{2,1,0:T(8,128)(2,1)S(1)}, u32[]{:S(2)}, u32[]{:S(2)}) async-start(bf16[4,24,2432]{2,1,0:T(8,128)(2,1)} %broadcast_in_dim.19), calls=%async_computation | async-start | bytes 933888 | tf_op jit(solution)/shard_map/all_to_all | solution.py:197
  15.1 9.2 %all-to-all-done.refs_0_ = bf16[4,24,2432]{2,1,0:T(8,128)(2,1)S(1)} async-done(((bf16[4,24,2432]{2,1,0:T(8,128)(2,1)}), bf16[4,24,2432]{2,1,0:T(8,128)(2,1)S(1)}, u32[]{:S(2)}, u32[]{:S(2)}) %all-to-all-start) | async-done | bytes 466976 | tf_op jit(solution)/shard_map/all_to_all | solution.py:197
  44.7 8.5 %collective-permute-done.4.refs_2_ = bf16[4,24,2432]{2,1,0:T(8,128)(2,1)} collective-permute-done((bf16[4,24,2432]{2,1,0:T(8,128)(2,1)S(1)}, bf16[4,24,2432]{2,1,0:T(8,128)(2,1)}, u32[]{:S(2)}, u32[]{:S(2)}) %collective-permute-start.4) | collective-permute-done | bytes 466976 | tf_op jit(solution)/shard_map/ppermute | solution.py:193
  58.3 5.0 %all-to-all-start.2 = ((bf16[4,24,2048]{2,1,0:T(8,128)(2,1)}), bf16[4,24,2048]{2,1,0:T(8,128)(2,1)S(1)}, u32[]{:S(2)}, u32[]{:S(2)}) async-start(bf16[4,24,2048]{2,1,0:T(8,128)(2,1)} %broadcast_in_dim.21), calls=%async_computation.2 | async-start | bytes 786432 | tf_op jit(solution)/shard_map/all_to_all | solution.py:197
  70.6 9.3 %qkv.1 = (bf16[1024,768]{1,0:T(8,128)(2,1)}, bf16[1024,768]{1,0:T(8,128)(2,1)}, bf16[1024,768]{1,0:T(8,128)(2,1)}, bf16[1024,768]{1,0:T(8,128)(2,1)}) custom-call(bf16[1024,768]{1,0:T(8,128)(2,1)} %bitcast.281, bf16[1,768]{1,0:T(2,128)(2,1)} %bitcast.312, f32[1024,128]{1,0:T(8,128)} %get-tuple-element.201.cos_ref, f32[1024,128]{1,0:T(8,128)} %get-tuple-element.202.sin_ref, ...), custom_call_target="tpu_custom_call" | custom-call | flops 3623878656 | bytes 11403264 | tf_op jit(solution)/shard_map/qkv/pallas_call | solution.py:57
  82.9 5.5 %all-to-all-start.3 = ((bf16[4,64,768]{2,1,0:T(8,128)(2,1)}), bf16[4,64,768]{2,1,0:T(8,128)(2,1)S(1)}, u32[]{:S(2)}, u32[]{:S(2)}) async-start(bf16[4,64,768]{2,1,0:T(8,128)(2,1)} %broadcast_in_dim.22), calls=%async_computation.3 | async-start | bytes 786432 | tf_op jit(solution)/shard_map/all_to_all | solution.py:197
  94.2 12.7 %attn_fwd.2 = (f32[1024,768]{1,0:T(8,128)}, bf16[1024,768]{1,0:T(8,128)(2,1)}, f32[6,2,1024]{2,1,0:T(2,128)}) custom-call(f32[9,256,256]{2,1,0:T(8,128)} %bias.1.bias_ref, bf16[1024,768]{1,0:T(8,128)(2,1)} %get-tuple-element.71.q_ref, bf16[1024,768]{1,0:T(8,128)(2,1)} %get-tuple-element.65.k_ref, bf16[1024,768]{1,0:T(8,128)(2,1)} %get-tuple-element.66.v_ref), custom_call_target="tpu_custom_call" | custom-call | flops 3623878656 | bytes 4718592 | tf_op jit(solution)/shard_map/attn_fwd/pallas_call | solution.py:114
  106.9 12.8 %attn_fwd.3 = (f32[1024,768]{1,0:T(8,128)}, bf16[1024,768]{1,0:T(8,128)(2,1)}, f32[6,2,1024]{2,1,0:T(2,128)}) custom-call(f32[9,256,256]{2,1,0:T(8,128)} %bias.1.bias_ref, bf16[1024,768]{1,0:T(8,128)(2,1)} %get-tuple-element.71.q_ref, bf16[1024,768]{1,0:T(8,128)(2,1)} %get-tuple-element.65.k_ref, ...), custom_call_target="tpu_custom_call", output_to_operand_aliasing={{0}: (4, {}), {1}: (5, {}), {2}: (6, {})} | custom-call | flops 3623878656 | bytes 4718592 | tf_op jit(solution)/shard_map/attn_fwd/pallas_call | solution.py:114
  127.5 4.9 %collective-permute-done.18 = bf16[4,64,768]{2,1,0:T(8,128)(2,1)} collective-permute-done((bf16[4,64,768]{2,1,0:T(8,128)(2,1)S(1)}, bf16[4,64,768]{2,1,0:T(8,128)(2,1)}, u32[]{:S(2)}, u32[]{:S(2)}) %collective-permute-start.18) | collective-permute-done | bytes 393248 | tf_op jit(solution)/shard_map/ppermute | solution.py:193
  151.6 5.7 %fusion.80 = f32[1024,2048]{1,0:T(8,128)} fusion(bf16[1024,768]{1,0:T(8,128)(2,1)S(1)} %multiply_convert_fusion.3, bf16[768,2048]{1,0:T(8,128)(2,1)S(1)} %bitcast.283), kind=kOutput, calls=%fused_computation.237 | convolution fusion | flops 3221225472 | bytes 13107200 | tf_op jit(solution)/shard_map/dot_general | solution.py:18
  158.2 5.7 %fusion.81 = f32[1024,2048]{1,0:T(8,128)} fusion(bf16[1024,768]{1,0:T(8,128)(2,1)S(1)} %multiply_convert_fusion.3, bf16[768,2048]{1,0:T(8,128)(2,1)S(1)} %bitcast.318), kind=kOutput, calls=%fused_computation.238 | convolution fusion | flops 3221225472 | bytes 13107200 | tf_op jit(solution)/shard_map/dot_general | solution.py:18
  167.8 13.7 %multiply_convert_fusion = (bf16[1024,2048]{1,0:T(8,128)(2,1)}, bf16[1024,2048]{1,0:T(8,128)(2,1)}, bf16[1024,2048]{1,0:T(8,128)(2,1)S(1)}) fusion(f32[1024,2048]{1,0:T(8,128)} %fusion.81, f32[1024,2048]{1,0:T(8,128)} %fusion.80, bf16[1024,768]{1,0:T(8,128)(2,1)} %bitcast.18, bf16[2048,768]{1,0:T(8,128)(2,1)} %bitcast.285), kind=kOutput, calls=%fused_computation | convolution fusion | flops 3250585600 | bytes 34078720 | tf_op jit(solution)/shard_map/dot_general | solution.py:18
  181.5 5.2 %convolution_convert_fusion.4 = bf16[2048,768]{1,0:T(8,128)(2,1)S(1)} fusion(bf16[1024,2048]{1,0:T(8,128)(2,1)S(1)} %get-tuple-element.111, bf16[1024,768]{1,0:T(8,128)(2,1)} %bitcast.18), kind=kOutput, calls=%fused_computation.14 | convolution fusion | flops 3222798336 | bytes 8912896 | tf_op jit(solution)/shard_map/dot_general | solution.py:18
  203.2 7.3 %fusion.82 = f32[1024,768]{1,0:T(8,128)} fusion(bf16[1024,2048]{1,0:T(8,128)(2,1)} %get-tuple-element.89, bf16[768,2048]{1,0:T(8,128)(2,1)S(1)} %bitcast.284), kind=kOutput, calls=%fused_computation.239 | convolution fusion | flops 3221225472 | bytes 10485760 | tf_op jit(solution)/shard_map/dot_general | solution.py:18
  210.5 9.1 %all-to-all-done.5 = bf16[4,256,768]{2,1,0:T(8,128)(2,1)} async-done(((bf16[4,256,768]{2,1,0:T(8,128)(2,1)}), bf16[4,256,768]{2,1,0:T(8,128)(2,1)}, u32[]{:S(2)}, u32[]{:S(2)}) %all-to-all-start.5) | async-done | bytes 1572896 | tf_op jit(solution)/shard_map/all_to_all | solution.py:197
  222.5 6.2 %convolution_convert_fusion.3 = bf16[768,2048]{1,0:T(8,128)(2,1)S(1)} fusion(bf16[1024,768]{1,0:T(8,128)(2,1)S(1)} %copy-done.17, bf16[1024,2048]{1,0:T(8,128)(2,1)} %get-tuple-element.90), kind=kOutput, calls=%fused_computation.13 | convolution fusion | flops 3222798336 | bytes 8912896 | tf_op jit(solution)/shard_map/dot_general | solution.py:18
  249.7 7.1 %collective-permute-done.28 = bf16[4,64,768]{2,1,0:T(8,128)(2,1)S(1)} collective-permute-done((bf16[4,64,768]{2,1,0:T(8,128)(2,1)S(1)}, bf16[4,64,768]{2,1,0:T(8,128)(2,1)S(1)}, u32[]{:S(2)}, u32[]{:S(2)}) %collective-permute-start.28) | collective-permute-done | bytes 393248 | tf_op jit(solution)/shard_map/ppermute | solution.py:193
  257.7 5.6 %all-to-all-start.6 = ((bf16[4,64,768]{2,1,0:T(8,128)(2,1)}), bf16[4,64,768]{2,1,0:T(8,128)(2,1)S(1)}, u32[]{:S(2)}, u32[]{:S(2)}) async-start(bf16[4,64,768]{2,1,0:T(8,128)(2,1)} %add_convert_fusion.2), calls=%async_computation.6 | async-start | bytes 786432 | tf_op jit(solution)/shard_map/all_to_all | solution.py:197
  280.4 6.1 %collective-permute-done.26 = bf16[4,2,24,2048]{3,2,0,1:T(8,128)(2,1)} collective-permute-done((bf16[4,2,24,2048]{3,2,0,1:T(8,128)(2,1)}, bf16[4,2,24,2048]{3,2,0,1:T(8,128)(2,1)}, u32[]{:S(2)}, u32[]{:S(2)}) %collective-permute-start.26) | collective-permute-done | bytes 786464 | tf_op jit(solution)/shard_map/ppermute | solution.py:193
  289.1 18.2 %attn_bwd.2 = bf16[1024,1152]{1,0:T(8,128)(2,1)} custom-call(f32[9,256,256]{2,1,0:T(8,128)} %bias.1.bias_ref, f32[1024,128]{1,0:T(8,128)} %get-tuple-element.201.cos_ref, f32[1024,128]{1,0:T(8,128)} %get-tuple-element.202.sin_ref, bf16[1024,768]{1,0:T(8,128)(2,1)} %get-tuple-element.71.q_ref, bf16[1024,768]{1,0:T(8,128)(2,1)} %get-tuple-element.65.k_ref, ...), custom_call_target="tpu_custom_call" | custom-call | flops 9059696640 | bytes 7077888 | tf_op jit(solution)/shard_map/attn_bwd/pallas_call | solution.py:177
  327.5 18.3 %attn_bwd.3 = bf16[1024,1152]{1,0:T(8,128)(2,1)} custom-call(f32[9,256,256]{2,1,0:T(8,128)} %bias.1.bias_ref, f32[1024,128]{1,0:T(8,128)} %get-tuple-element.201.cos_ref, f32[1024,128]{1,0:T(8,128)} %get-tuple-element.202.sin_ref, bf16[1024,768]{1,0:T(8,128)(2,1)} %get-tuple-element.71.q_ref, bf16[1024,768]{1,0:T(8,128)(2,1)} %get-tuple-element.65.k_ref, ...), custom_call_target="tpu_custom_call" | custom-call | flops 9059696640 | bytes 7077888 | tf_op jit(solution)/shard_map/attn_bwd/pallas_call | solution.py:177
  345.8 6.3 %fusion.10 = (f32[768]{0:T(1024)S(1)}, f32[1024]{0:T(1024)S(1)}, f32[1024,768]{1,0:T(8,128)S(1)}) fusion(f32[1024]{0:T(1024)S(1)} %bitcast.310, bf16[4,256,768]{2,1,0:T(8,128)(2,1)} %slice.236, f32[768]{0:T(1024)S(1)} %convert_reduce_fusion, f32[1024,768]{1,0:T(8,128)} %fusion.14, bf16[1024,1152]{1,0:T(8,128)(2,1)} %attn_bwd.3, bf16[768,2304]{1,0:T(8,128)(2,1)} %bitcast.316), kind=kOutput, calls=%fused_computation.22 | convolution fusion | flops 1818228992 | bytes 12007424 | tf_op jit(solution)/shard_map/dot_general | solution.py:18
  385.0 6.1 %collective-permute-done.37 = bf16[1,24,6016]{2,1,0:T(8,128)(2,1)} collective-permute-done((bf16[1,24,6016]{2,1,0:T(8,128)(2,1)}, bf16[1,24,6016]{2,1,0:T(8,128)(2,1)}, u32[]{:S(2)}, u32[]{:S(2)}) %collective-permute-start.37) | collective-permute-done | bytes 288800 | tf_op jit(solution)/shard_map/ppermute | solution.py:281
  394.7 5.0 %collective-permute-start.42 = (bf16[1,24,1280]{2,1,0:T(8,128)(2,1)S(1)}, bf16[1,24,1280]{2,1,0:T(8,128)(2,1)S(1)}, u32[]{:S(2)}, u32[]{:S(2)}) collective-permute-start(bf16[1,24,1280]{2,1,0:T(8,128)(2,1)S(1)} %get-tuple-element.149), channel_id=1, source_target_pairs={{0,8},{8,16},{16,24},{24,0},{1,9},{9,17},{17,25},{25,1},{2,10},{10... | collective-permute-start | bytes 184328 | tf_op jit(solution)/shard_map/ppermute | solution.py:281
  (316 shorter events, 212.7 us)
Async XLA Ops:
  13.6 23.5 %collective-permute-start.1 = (bf16[1,264,768]{2,1,0:T(8,128)(2,1)S(1)}, bf16[1,264,768]{2,1,0:T(8,128)(2,1)S(1)}, u32[]{:S(2)}, u32[]{:S(2)}) collective-permute-start(bf16[1,264,768]{2,1,0:T(8,128)(2,1)S(1)} %get-tuple-element.137), channel_id=1, source_target_pairs={{0,2},{1,3},{2,0},{3,1},{4,6},{5,7},{6,4},{7,5},{8,10},{9,11},{10,... | collective-permute-start | bytes 1216520 | tf_op jit(solution)/shard_map/ppermute | solution.py:206
  14.4 22.7 %collective-permute-start = (bf16[1,264,768]{2,1,0:T(8,128)(2,1)S(1)}, bf16[1,264,768]{2,1,0:T(8,128)(2,1)S(1)}, u32[]{:S(2)}, u32[]{:S(2)}) collective-permute-start(bf16[1,264,768]{2,1,0:T(8,128)(2,1)S(1)} %get-tuple-element.138), channel_id=1, source_target_pairs={{0,1},{1,0},{2,3},{3,2},{4,5},{5,4},{6,7},{7,6},{8,9},{9,8},{10,11... | collective-permute-start | bytes 1216520 | tf_op jit(solution)/shard_map/ppermute | solution.py:206
  31.7 21.5 %collective-permute-start.4 = (bf16[4,24,2432]{2,1,0:T(8,128)(2,1)S(1)}, bf16[4,24,2432]{2,1,0:T(8,128)(2,1)}, u32[]{:S(2)}, u32[]{:S(2)}) collective-permute-start(bf16[4,24,2432]{2,1,0:T(8,128)(2,1)S(1)} %all-to-all-done.refs_0_), channel_id=1, source_target_pairs={{0,4},{4,0},{1,5},{5,1},{2,6},{6,2},{3,7},{7,3},{8,12},{12,8},{9,1... | collective-permute-start | bytes 1400840 | tf_op jit(solution)/shard_map/ppermute | solution.py:193
  32.2 21.4 %collective-permute-start.3 = (bf16[4,24,2432]{2,1,0:T(8,128)(2,1)S(1)}, bf16[4,24,2432]{2,1,0:T(8,128)(2,1)}, u32[]{:S(2)}, u32[]{:S(2)}) collective-permute-start(bf16[4,24,2432]{2,1,0:T(8,128)(2,1)S(1)} %all-to-all-done.refs_0_), channel_id=1, source_target_pairs={{0,2},{2,0},{1,3},{3,1},{4,6},{6,4},{5,7},{7,5},{8,10},{10,8},{9,1... | collective-permute-start | bytes 1400840 | tf_op jit(solution)/shard_map/ppermute | solution.py:193
  44.2 20.1 %collective-permute-start.6 = (bf16[4,24,2432]{2,1,0:T(8,128)(2,1)S(1)}, bf16[4,24,2432]{2,1,0:T(8,128)(2,1)}, u32[]{:S(2)}, u32[]{:S(2)}) collective-permute-start(bf16[4,24,2432]{2,1,0:T(8,128)(2,1)S(1)} %all-to-all-done.refs_0_), channel_id=1, source_target_pairs={{0,1},{1,0},{2,3},{3,2},{4,5},{5,4},{6,7},{7,6},{8,9},{9,8},{10,11... | collective-permute-start | bytes 1400840 | tf_op jit(solution)/shard_map/ppermute | solution.py:193
  58.3 21.6 %all-to-all-start.2 = ((bf16[4,24,2048]{2,1,0:T(8,128)(2,1)}), bf16[4,24,2048]{2,1,0:T(8,128)(2,1)S(1)}, u32[]{:S(2)}, u32[]{:S(2)}) async-start(bf16[4,24,2048]{2,1,0:T(8,128)(2,1)} %broadcast_in_dim.21), calls=%async_computation.2 | async-start | bytes 786432 | tf_op jit(solution)/shard_map/all_to_all | solution.py:197
  81.5 38.2 %collective-permute-start.12 = (bf16[8,24,2816]{2,1,0:T(8,128)(2,1)S(1)}, bf16[8,24,2816]{2,1,0:T(8,128)(2,1)}, u32[]{:S(2)}, u32[]{:S(2)}) collective-permute-start(bf16[8,24,2816]{2,1,0:T(8,128)(2,1)S(1)} %constant_dynamic-update-slice_fusion.refs_0_), channel_id=1, source_target_pairs={{0,4},{4,0},{1,5},{5,1},{2,6},{6,2},{3,7},{7,3},{8,12},{12,8},{9,1... | collective-permute-start | bytes 3244040 | tf_op jit(solution)/shard_map/ppermute | solution.py:193
  82.1 57.5 %collective-permute-start.13 = (bf16[8,24,2816]{2,1,0:T(8,128)(2,1)S(1)}, bf16[8,24,2816]{2,1,0:T(8,128)(2,1)}, u32[]{:S(2)}, u32[]{:S(2)}) collective-permute-start(bf16[8,24,2816]{2,1,0:T(8,128)(2,1)S(1)} %constant_dynamic-update-slice_fusion.refs_0_), channel_id=1, source_target_pairs={{0,1},{1,0},{2,3},{3,2},{4,5},{5,4},{6,7},{7,6},{8,9},{9,8},{10,11... | collective-permute-start | bytes 3244040 | tf_op jit(solution)/shard_map/ppermute | solution.py:193
  82.9 24.0 %all-to-all-start.3 = ((bf16[4,64,768]{2,1,0:T(8,128)(2,1)}), bf16[4,64,768]{2,1,0:T(8,128)(2,1)S(1)}, u32[]{:S(2)}, u32[]{:S(2)}) async-start(bf16[4,64,768]{2,1,0:T(8,128)(2,1)} %broadcast_in_dim.22), calls=%async_computation.3 | async-start | bytes 786432 | tf_op jit(solution)/shard_map/all_to_all | solution.py:197
  93.1 27.2 %collective-permute-start.15 = (bf16[8,24,2048]{2,1,0:T(8,128)(2,1)S(1)}, bf16[8,24,2048]{2,1,0:T(8,128)(2,1)}, u32[]{:S(2)}, u32[]{:S(2)}) collective-permute-start(bf16[8,24,2048]{2,1,0:T(8,128)(2,1)S(1)} %constant_dynamic-update-slice_fusion.2.refs_0_), channel_id=1, source_target_pairs={{0,2},{2,0},{1,3},{3,1},{4,6},{6,4},{5,7},{7,5},{8,10},{10,8},{9,1... | collective-permute-start | bytes 2359304 | tf_op jit(solution)/shard_map/ppermute | solution.py:193
  119.7 20.0 %collective-permute-start.14 = (bf16[8,24,2816]{2,1,0:T(8,128)(2,1)}, bf16[8,24,2816]{2,1,0:T(8,128)(2,1)S(1)}, u32[]{:S(2)}, u32[]{:S(2)}) collective-permute-start(bf16[8,24,2816]{2,1,0:T(8,128)(2,1)} %collective-permute-done.12.refs_1_), channel_id=1, source_target_pairs={{0,1},{1,0},{2,3},{3,2},{4,5},{5,4},{6,7},{7,6},{8,9},{9,8},{10,11... | collective-permute-start | bytes 3244040 | tf_op jit(solution)/shard_map/ppermute | solution.py:193
  122.1 45.7 %all-to-all-start.4 = ((bf16[4,256,768]{2,1,0:T(8,128)(2,1)}), bf16[4,256,768]{2,1,0:T(8,128)(2,1)}, u32[]{:S(2)}, u32[]{:S(2)}) async-start(bf16[4,256,768]{2,1,0:T(8,128)(2,1)} %bitcast.17), calls=%async_computation.4 | async-start | bytes 3145728 | tf_op jit(solution)/shard_map/all_to_all | solution.py:197
  134.2 23.1 %collective-permute-start.19 = (bf16[8,64,768]{2,1,0:T(8,128)(2,1)}, bf16[8,64,768]{2,1,0:T(8,128)(2,1)}, u32[]{:S(2)}, u32[]{:S(2)}) collective-permute-start(bf16[8,64,768]{2,1,0:T(8,128)(2,1)} %constant_dynamic-update-slice_fusion.4.refs_0_), channel_id=1, source_target_pairs={{0,4},{4,0},{1,5},{5,1},{2,6},{6,2},{3,7},{7,3},{8,12},{12,8},{9,1... | collective-permute-start | bytes 2359304 | tf_op jit(solution)/shard_map/ppermute | solution.py:193
  135.8 28.1 %collective-permute-start.20 = (bf16[8,64,768]{2,1,0:T(8,128)(2,1)}, bf16[8,64,768]{2,1,0:T(8,128)(2,1)}, u32[]{:S(2)}, u32[]{:S(2)}) collective-permute-start(bf16[8,64,768]{2,1,0:T(8,128)(2,1)} %constant_dynamic-update-slice_fusion.4.refs_0_), channel_id=1, source_target_pairs={{0,1},{1,0},{2,3},{3,2},{4,5},{5,4},{6,7},{7,6},{8,9},{9,8},{10,11... | collective-permute-start | bytes 2359304 | tf_op jit(solution)/shard_map/ppermute | solution.py:193
  188.0 31.6 %collective-permute-start.22 = (bf16[4,2,2,64,768]{4,3,0,2,1:T(8,128)(2,1)}, bf16[4,2,2,64,768]{4,3,0,2,1:T(8,128)(2,1)}, u32[]{:S(2)}, u32[]{:S(2)}) collective-permute-start(bf16[4,2,2,64,768]{4,3,0,2,1:T(8,128)(2,1)} %copy_bitcast_fusion.2), channel_id=1, source_target_pairs={{0,1},{1,0},{2,3},{3,2},{4,5},{5,4},{6,7},{7,6},{8,9},{9,8},{10,11... | collective-permute-start | bytes 4718600 | tf_op jit(solution)/shard_map/ppermute | solution.py:193
  194.7 24.9 %all-to-all-start.5 = ((bf16[4,256,768]{2,1,0:T(8,128)(2,1)}), bf16[4,256,768]{2,1,0:T(8,128)(2,1)}, u32[]{:S(2)}, u32[]{:S(2)}) async-start(bf16[4,256,768]{2,1,0:T(8,128)(2,1)} %bitcast.300), calls=%async_computation.5 | async-start | bytes 3145728 | tf_op jit(solution)/shard_map/all_to_all | solution.py:197
  222.0 19.8 %collective-permute-start.24 = (bf16[4,2,64,768]{3,2,0,1:T(8,128)(2,1)S(1)}, bf16[4,2,64,768]{3,2,0,1:T(8,128)(2,1)S(1)}, u32[]{:S(2)}, u32[]{:S(2)}) collective-permute-start(bf16[4,2,64,768]{3,2,0,1:T(8,128)(2,1)S(1)} %get-tuple-element.143), channel_id=1, source_target_pairs={{0,4},{4,0},{1,5},{5,1},{2,6},{6,2},{3,7},{7,3},{8,12},{12,8},{9,1... | collective-permute-start | bytes 2359304 | tf_op jit(solution)/shard_map/ppermute | solution.py:193
  245.1 30.5 %collective-permute-start.25 = (bf16[4,2,2,24,2816]{4,3,0,1,2:T(8,128)(2,1)}, bf16[4,2,2,24,2816]{4,3,0,1,2:T(8,128)(2,1)}, u32[]{:S(2)}, u32[]{:S(2)}) collective-permute-start(bf16[4,2,2,24,2816]{4,3,0,1,2:T(8,128)(2,1)} %pad_maximum_fusion), channel_id=1, source_target_pairs={{0,1},{1,0},{2,3},{3,2},{4,5},{5,4},{6,7},{7,6},{8,9},{9,8},{10,11... | collective-permute-start | bytes 6488072 | tf_op jit(solution)/shard_map/ppermute | solution.py:193
  280.1 27.2 %collective-permute-start.27 = (bf16[4,2,24,2816]{3,2,0,1:T(8,128)(2,1)}, bf16[4,2,24,2816]{3,2,0,1:T(8,128)(2,1)}, u32[]{:S(2)}, u32[]{:S(2)}) collective-permute-start(bf16[4,2,24,2816]{3,2,0,1:T(8,128)(2,1)} %get-tuple-element.127), channel_id=1, source_target_pairs={{0,2},{2,0},{1,3},{3,1},{4,6},{6,4},{5,7},{7,5},{8,10},{10,8},{9,1... | collective-permute-start | bytes 3244040 | tf_op jit(solution)/shard_map/ppermute | solution.py:193
  288.7 24.6 %collective-permute-start.30 = (bf16[4,24,2048]{2,1,0:T(8,128)(2,1)S(1)}, bf16[4,24,2048]{2,1,0:T(8,128)(2,1)S(1)}, u32[]{:S(2)}, u32[]{:S(2)}) collective-permute-start(bf16[4,24,2048]{2,1,0:T(8,128)(2,1)S(1)} %get-tuple-element.125), channel_id=1, source_target_pairs={{0,2},{2,0},{1,3},{3,1},{4,6},{6,4},{5,7},{7,5},{8,10},{10,8},{9,1... | collective-permute-start | bytes 1179656 | tf_op jit(solution)/shard_map/ppermute | solution.py:193
  324.0 21.8 %collective-permute-start.33 = (bf16[4,24,1152]{2,1,0:T(8,128)(2,1)}, bf16[4,24,1152]{2,1,0:T(8,128)(2,1)S(1)}, u32[]{:S(2)}, u32[]{:S(2)}) collective-permute-start(bf16[4,24,1152]{2,1,0:T(8,128)(2,1)} %get-tuple-element.122), channel_id=1, source_target_pairs={{0,4},{4,0},{1,5},{5,1},{2,6},{6,2},{3,7},{7,3},{8,12},{12,8},{9,1... | collective-permute-start | bytes 663560 | tf_op jit(solution)/shard_map/ppermute | solution.py:193
  325.3 20.4 %collective-permute-start.34 = (bf16[4,24,1152]{2,1,0:T(8,128)(2,1)}, bf16[4,24,1152]{2,1,0:T(8,128)(2,1)S(1)}, u32[]{:S(2)}, u32[]{:S(2)}) collective-permute-start(bf16[4,24,1152]{2,1,0:T(8,128)(2,1)} %get-tuple-element.121), channel_id=1, source_target_pairs={{0,6},{2,4},{4,2},{6,0},{1,7},{3,5},{5,3},{7,1},{8,14},{10,12},{12... | collective-permute-start | bytes 663560 | tf_op jit(solution)/shard_map/ppermute | solution.py:286
  359.1 45.3 %all-to-all-start.7 = ((bf16[4,256,768]{2,1,0:T(8,128)(2,1)}), bf16[4,256,768]{2,1,0:T(8,128)(2,1)S(1)}, u32[]{:S(2)}, u32[]{:S(2)}) async-start(bf16[4,256,768]{2,1,0:T(8,128)(2,1)} %bitcast.57), calls=%async_computation.7 | async-start | bytes 3145728 | tf_op jit(solution)/shard_map/all_to_all | solution.py:197
  370.5 20.6 %collective-permute-start.37 = (bf16[1,24,6016]{2,1,0:T(8,128)(2,1)}, bf16[1,24,6016]{2,1,0:T(8,128)(2,1)}, u32[]{:S(2)}, u32[]{:S(2)}) collective-permute-start(bf16[1,24,6016]{2,1,0:T(8,128)(2,1)} %pad_maximum_fusion.6), channel_id=1, source_target_pairs={{0,24},{8,0},{16,8},{24,16},{1,25},{9,1},{17,9},{25,17},{2,26},{10... | collective-permute-start | bytes 866312 | tf_op jit(solution)/shard_map/ppermute | solution.py:281
  (81 other events, 723.9 us)
